TPU v7x, 256 devices: a whole 4x4x8 slice. The times are simulated.
256 devices in a mesh: isl: 16 (over z_lo, x), par: 2 (over z_hi), sp: 8 (over y, core).
Axes of the slice: x: 4, y: 4, z: 8 (z_hi: 2, z_lo: 4; z = z_hi * 4 + z_lo), core: 2. Of those that a mesh axis runs over, the one named last changes fastest.
Arguments:
- ensemble: float32 [16, 2, 4, 32, 32, 512], P('isl', 'par', None, 'sp'), may hold values from -6 to 6
- observations: float32 [32, 512], P('sp'), may hold values from -6 to 6
- obs_precision: float32 [32, 512], P('sp'), may hold values from 0.002 to 0.02
- island_ancestor: int32 [16], replicated, may hold values from 0 to 15, as said below
- particle_ancestor: int32 [16, 2], P('isl', 'par'), may hold values from 0 to 1, as said below
Outputs:
- resampled: float32 [16, 2, 4, 32, 32, 512], P('isl', 'par', None, 'sp')
- particle_logw: float32 [16, 2], P('isl', 'par')
- island_logw: float32 [16], P('isl')
Inputs may be any that keep to these rules, and one draw needn't show every extreme that they name: island_ancestor names island 16 - 1 and island 0 in every draw. Every row of particle_ancestor names particle 0 and particle 2 - 1.
All inputs are finite; a program needn't handle non-finite values.
Results may differ from a plain program's by a relative error of at most 0.000069.
Values sent between devices are 32-bit elements; how exact they have to be, the bound alone decides.
A program may use at most 64 MiB of HBM per device.

v0:
```python
import jax
import jax.numpy as jnp
from jax import lax
from jax.sharding import PartitionSpec as P

SWEEPS = 8


dt_step = 0.2
viscosity = 0.05
stratification = 1.0
relaxation = 0.8


def extended_2(cells, sides, width):
    for axis, dim in sides:
        count = lax.axis_size(axis)
        head = lax.slice_in_dim(cells, 0, width, axis=dim)
        tail = lax.slice_in_dim(cells, cells.shape[dim] - width, cells.shape[dim], axis=dim)
        cells = jnp.concatenate(
            [
                lax.ppermute(tail, axis, [(i, (i + 1) % count) for i in range(count)]),
                cells,
                lax.ppermute(head, axis, [((i + 1) % count, i) for i in range(count)]),
            ],
            axis=dim,
        )
    return cells


def pad_vertical(field, width):
    pad_widths = [(0, 0)] * field.ndim
    pad_widths[-2] = (width, width)
    return jnp.pad(field, pad_widths)


def fourth_north(field):
    return (
        8.0 * (jnp.roll(field, -1, -1) - jnp.roll(field, 1, -1))
        - (jnp.roll(field, -2, -1) - jnp.roll(field, 2, -1))
    ) / 12.0


def fourth_vertical(field):
    padded = pad_vertical(field, 2)
    return (
        8.0 * (padded[..., 3:-1, :] - padded[..., 1:-3, :])
        - (padded[..., 4:, :] - padded[..., :-4, :])
    ) / 12.0


def fourth_east(extended):
    return (
        8.0 * (extended[..., 3:-1, :, :] - extended[..., 1:-3, :, :])
        - (extended[..., 4:, :, :] - extended[..., :-4, :, :])
    ) / 12.0


def second_north(field):
    return 0.5 * (jnp.roll(field, -1, -1) - jnp.roll(field, 1, -1))


def second_vertical(field):
    padded = pad_vertical(field, 1)
    return 0.5 * (padded[..., 2:, :] - padded[..., :-2, :])


def centred_east(padded):
    return 0.5 * (padded[..., 2:, :, :] - padded[..., :-2, :, :])


def neighbours(padded):
    middle = padded[..., 1:-1, :, :]
    vertical = pad_vertical(middle, 1)
    return (
        padded[..., 2:, :, :]
        + padded[..., :-2, :, :]
        + jnp.roll(middle, 1, -1)
        + jnp.roll(middle, -1, -1)
        + vertical[..., 2:, :]
        + vertical[..., :-2, :]
    )


def tendency(extended, zonal, merid, vertical_flow):
    field = extended[..., 2:-2, :, :]
    laplace = neighbours(extended[..., 1:-1, :, :]) - 6.0 * field
    advect = (
        zonal * fourth_east(extended)
        + merid * fourth_north(field)
        + vertical_flow * fourth_vertical(field)
    )
    return viscosity * laplace - advect


def sweep(padded, divergence):
    middle = padded[..., 1:-1, :, :]
    return middle + relaxation * (neighbours(padded) - 6.0 * middle - divergence) / 6.0


def log_total(values, axis_index):
    upper_boundary = jnp.max(values, axis=axis_index, keepdims=True)
    return jnp.squeeze(upper_boundary, axis_index) + jnp.log(
        jnp.sum(jnp.exp(values - upper_boundary), axis=axis_index)
    )


def shards(ensemble, observations, obs_precision, island_ancestor, particle_ancestor):
    model_state = ensemble[0]
    rows_east = model_state.shape[2]
    island_now = lax.axis_index("isl")
    source_island = island_ancestor[island_now]
    picks = particle_ancestor[0]
    zonal = model_state[:, 0]
    merid = model_state[:, 1]
    vertical_flow = model_state[:, 2]
    buoyancy = model_state[:, 3]
    extended = extended_2(model_state, (("sp", 2),), 2)
    star_zonal = zonal + dt_step * tendency(extended[:, 0], zonal, merid, vertical_flow)
    star_merid = merid + dt_step * tendency(extended[:, 1], zonal, merid, vertical_flow)
    star_vertical = vertical_flow + dt_step * (
        tendency(extended[:, 2], zonal, merid, vertical_flow) + buoyancy
    )
    buoyancy_provisional_tendency = buoyancy + dt_step * (
        tendency(extended[:, 3], zonal, merid, vertical_flow) - stratification * vertical_flow
    )
    zonal_wide = extended_2(star_zonal, (("sp", 1),), 1)
    divergence = (
        centred_east(zonal_wide) + second_north(star_merid) + second_vertical(star_vertical)
    )
    potential = -relaxation * divergence / 6.0
    for repeat_index in range(SWEEPS):
        padded = extended_2(potential, (("sp", 1),), 1)
        potential = sweep(padded, divergence)
    padded = extended_2(potential, (("sp", 1),), 1)
    stepped = jnp.stack(
        [
            star_zonal - centred_east(padded),
            star_merid - second_north(potential),
            star_vertical - second_vertical(potential),
            buoyancy_provisional_tendency,
        ],
        axis=1,
    )
    upper_boundary = stepped[:, 3][:, :, -1, :]
    nx_total = lax.axis_size("sp") * rows_east
    positions = (lax.axis_index("sp") * rows_east + jnp.arange(rows_east, dtype=jnp.int32)).astype(
        jnp.float32
    )
    ramp = 1.0 + positions * (2.0 / (nx_total - 1))
    scale = obs_precision * ramp[:, None]
    partial_value = jnp.sum((upper_boundary - observations) ** 2 * scale, axis=(1, 2))
    misfit = lax.psum(partial_value, "sp")
    log_weight = -0.5 * misfit
    island_weights = lax.all_gather(log_weight, "par", axis=0, tiled=True)
    island_total = log_total(island_weights, 0)
    particle_out = log_weight - island_total
    totals = lax.all_gather(island_total[None], "isl", axis=0, tiled=True)
    island_out = island_total - log_total(totals, 0)
    particle_out, island_out = (particle_out, island_out)
    piece = lax.all_gather(stepped[None], "isl", axis=0, tiled=True)
    labels = jnp.arange(piece.shape[0], dtype=jnp.int32)
    matched = (labels == source_island)[:, None, None, None, None, None]
    copied = jnp.sum(jnp.where(matched, piece, 0.0), axis=0, keepdims=True)
    complete_island_state = lax.all_gather(copied, "par", axis=1, tiled=True)
    result = jnp.take(complete_island_state[0], picks, axis=0)
    return (result[None], particle_out[None], island_out[None])


def solution(mesh):
    return jax.shard_map(
        shards,
        mesh=mesh,
        in_specs=(
            P("isl", "par", None, "sp", None, None),
            P("sp", None),
            P("sp", None),
            P(),
            P("isl", "par"),
        ),
        out_specs=(P("isl", "par", None, "sp", None, None), P("isl", "par"), P("isl")),
        check_vma=False,
    )
```

profile of v0, /device:TPU:128, one launch (start us, length us, event | category | flops | bytes accessed | tf_op | source)
XLA Modules:
  0.0 370.2 jit_solution(13943572929849867741)
XLA Ops:
  7.2 1.4 fusion.178
  8.6 2.9 collective-permute-start.1
  11.6 6.9 %collective-permute-done = f32[1,4,2,32,512]{4,3,2,1,0:T(8,128)S(1)} collective-permute-done((f32[1,4,2,32,512]{4,3,2,1,0:T(8,128)S(1)}, f32[1,4,2,32,512]{4,3,2,1,0:T(8,128)S(1)}, u32[]{:S(2)}, u32[]{:S(2)}) %collective-permute-start) | collective-permute-done | bytes 524320 | tf_op jit(solution)/shard_map/ppermute | solution.py:22
  21.4 3.0 collective-permute-start.2
  26.2 3.0 collective-permute-done.3
  30.2 1.3 collective-permute-done.4
  31.5 3.0 collective-permute-done.5
  35.5 1.3 collective-permute-done.6
  36.8 3.0 collective-permute-done.7
  40.8 1.3 collective-permute-done.8
  42.1 3.0 collective-permute-done.9
  46.1 1.3 collective-permute-done.10
  47.4 3.0 collective-permute-done.11
  51.4 1.3 collective-permute-done.12
  52.7 3.0 collective-permute-done.13
  56.7 1.3 collective-permute-done.14
  58.1 3.0 collective-permute-done.15
  62.1 1.3 collective-permute-done.16
  63.4 3.0 collective-permute-done.17
  67.4 1.3 collective-permute-done.18
  68.7 3.0 collective-permute-done.19
  72.9 1.2 collective-permute-done.20
  74.1 3.0 collective-permute-done.21
  79.7 181.6 %all-gather.5.cloned.1.call-done = f32[16,4,4,32,512]{4,3,2,1,0:T(8,128)} async-done(((f32[1,4,4,32,512]{4,3,2,1,0:T(8,128)}), f32[16,4,4,32,512]{4,3,2,1,0:T(8,128)}) %all-gather.5.cloned.1.call-update) | async-done | bytes 16777232 | tf_op jit(solution)/shard_map/all_gather | solution.py:161
  261.3 9.1 %fusion = f32[4,4,32,512]{3,2,1,0:T(8,128)} fusion(f32[16,4,4,32,512]{4,3,2,1,0:T(8,128)} %all-gather.5.cloned.1.call-done, pred[16]{0:T(512)(128)(4,1)S(1)} %iota_compare_fusion), kind=kLoop, calls=%fused_computation.1 | loop fusion | flops 8126464 | bytes 17825808 | tf_op jit(solution)/shard_map/reduce_sum | solution.py:164
  273.0 15.0 %psum.7 = f32[1]{0:T(128)} all-reduce(f32[1]{0:T(128)} %bitcast.19), channel_id=1, replica_groups=mesh['isl'=16,'par'=2,'sp'=8] {'sp'}, use_global_device_ids=true, to_apply=%region_2.3 | all-reduce | flops 1 | bytes 8 | tf_op jit(solution)/shard_map/psum | solution.py:153
  288.0 1.4 multiply_dynamic-update-slice_fusion
  289.4 11.1 %all-reduce.18 = f32[2]{0:T(128)S(1)} all-reduce(f32[2]{0:T(128)S(1)} %multiply_dynamic-update-slice_fusion), channel_id=1, replica_groups=mesh['isl'=16,'par'=2,'sp'=8] {'par'}, use_global_device_ids=true, to_apply=%add.18 | all-reduce | flops 2 | bytes 16
  301.1 1.3 exponential_reduce_fusion.1
  304.4 50.6 %all-reduce.19 = f32[16]{0:T(128)S(1)} all-reduce(f32[16]{0:T(128)S(1)} %dynamic-update-slice.2), channel_id=1, replica_groups=mesh['isl'=16,'par'=2,'sp'=8] {'isl'}, use_global_device_ids=true, to_apply=%add.19 | all-reduce | flops 16 | bytes 128
  355.6 1.2 exponential_reduce_fusion
  358.8 2.3 dynamic-slice_select_fusion
  (111 shorter events, 19.8 us)
Async XLA Ops:
  7.2 11.3 %copy-start = (f32[1,1,4,4,32,512]{5,4,3,2,1,0:T(8,128)S(1)}, f32[1,1,4,4,32,512]{5,4,3,2,1,0:T(8,128)}, u32[]{:S(2)}) copy-start(f32[1,1,4,4,32,512]{5,4,3,2,1,0:T(8,128)} %param.5) | copy-start | bytes 3145732
  7.2 254.1 %all-gather.5.cloned.1.call-start = ((), (), s32[]{:S(2)}) async-start(), calls=%async_computation | async-start | bytes 17825792 | tf_op jit(solution)/shard_map/all_gather | solution.py:161
  8.6 9.8 %collective-permute-start = (f32[1,4,2,32,512]{4,3,2,1,0:T(8,128)S(1)}, f32[1,4,2,32,512]{4,3,2,1,0:T(8,128)S(1)}, u32[]{:S(2)}, u32[]{:S(2)}) collective-permute-start(f32[1,4,2,32,512]{4,3,2,1,0:T(8,128)S(1)} %get-tuple-element.20), channel_id=1, source_target_pairs={{0,1},{1,2},{2,3},{3,4},{4,5},{5,6},{6,7},{7,0},{8,9},{9,10},{10,1... | collective-permute-start | bytes 1572872 | tf_op jit(solution)/shard_map/ppermute | solution.py:22
  8.6 9.8 %collective-permute-start.1 = (f32[1,4,2,32,512]{4,3,2,1,0:T(8,128)S(1)}, f32[1,4,2,32,512]{4,3,2,1,0:T(8,128)S(1)}, u32[]{:S(2)}, u32[]{:S(2)}) collective-permute-start(f32[1,4,2,32,512]{4,3,2,1,0:T(8,128)S(1)} %get-tuple-element.21), channel_id=1, source_target_pairs={{1,0},{2,1},{3,2},{4,3},{5,4},{6,5},{7,6},{0,7},{9,8},{10,9},{11,1... | collective-permute-start | bytes 1572872 | tf_op jit(solution)/shard_map/ppermute | solution.py:24
  21.4 4.9 %collective-permute-start.2 = (f32[1,1,32,512]{3,2,1,0:T(8,128)S(1)}, f32[1,1,32,512]{3,2,1,0:T(8,128)S(1)}, u32[]{:S(2)}, u32[]{:S(2)}) collective-permute-start(f32[1,1,32,512]{3,2,1,0:T(8,128)S(1)} %get-tuple-element.110), channel_id=1, source_target_pairs={{1,0},{2,1},{3,2},{4,3},{5,4},{6,5},{7,6},{0,7},{9,8},{10,9},{11,1... | collective-permute-start | bytes 196616 | tf_op jit(solution)/shard_map/ppermute | solution.py:24
  24.3 4.9 %collective-permute-start.3 = (f32[1,1,32,512]{3,2,1,0:T(8,128)S(1)}, f32[1,1,32,512]{3,2,1,0:T(8,128)S(1)}, u32[]{:S(2)}, u32[]{:S(2)}) collective-permute-start(f32[1,1,32,512]{3,2,1,0:T(8,128)S(1)} %get-tuple-element.111), channel_id=1, source_target_pairs={{0,1},{1,2},{2,3},{3,4},{4,5},{5,6},{6,7},{7,0},{8,9},{9,10},{10,1... | collective-permute-start | bytes 196616 | tf_op jit(solution)/shard_map/ppermute | solution.py:22
  29.6 1.9 collective-permute-start.4
  29.6 4.9 %collective-permute-start.5 = (f32[1,1,32,512]{3,2,1,0:T(8,128)S(1)}, f32[1,1,32,512]{3,2,1,0:T(8,128)S(1)}, u32[]{:S(2)}, u32[]{:S(2)}) collective-permute-start(f32[1,1,32,512]{3,2,1,0:T(8,128)S(1)} %get-tuple-element.109), channel_id=1, source_target_pairs={{0,1},{1,2},{2,3},{3,4},{4,5},{5,6},{6,7},{7,0},{8,9},{9,10},{10,1... | collective-permute-start | bytes 196616 | tf_op jit(solution)/shard_map/ppermute | solution.py:22
  34.9 1.9 collective-permute-start.6
  34.9 4.9 %collective-permute-start.7 = (f32[1,1,32,512]{3,2,1,0:T(8,128)S(1)}, f32[1,1,32,512]{3,2,1,0:T(8,128)S(1)}, u32[]{:S(2)}, u32[]{:S(2)}) collective-permute-start(f32[1,1,32,512]{3,2,1,0:T(8,128)S(1)} %get-tuple-element.103), channel_id=1, source_target_pairs={{0,1},{1,2},{2,3},{3,4},{4,5},{5,6},{6,7},{7,0},{8,9},{9,10},{10,1... | collective-permute-start | bytes 196616 | tf_op jit(solution)/shard_map/ppermute | solution.py:22
  40.2 1.9 collective-permute-start.8
  40.2 4.9 %collective-permute-start.9 = (f32[1,1,32,512]{3,2,1,0:T(8,128)S(1)}, f32[1,1,32,512]{3,2,1,0:T(8,128)S(1)}, u32[]{:S(2)}, u32[]{:S(2)}) collective-permute-start(f32[1,1,32,512]{3,2,1,0:T(8,128)S(1)} %get-tuple-element.97), channel_id=1, source_target_pairs={{0,1},{1,2},{2,3},{3,4},{4,5},{5,6},{6,7},{7,0},{8,9},{9,10},{10,1... | collective-permute-start | bytes 196616 | tf_op jit(solution)/shard_map/ppermute | solution.py:22
  45.5 1.9 collective-permute-start.10
  45.5 4.9 %collective-permute-start.11 = (f32[1,1,32,512]{3,2,1,0:T(8,128)S(1)}, f32[1,1,32,512]{3,2,1,0:T(8,128)S(1)}, u32[]{:S(2)}, u32[]{:S(2)}) collective-permute-start(f32[1,1,32,512]{3,2,1,0:T(8,128)S(1)} %get-tuple-element.91), channel_id=1, source_target_pairs={{0,1},{1,2},{2,3},{3,4},{4,5},{5,6},{6,7},{7,0},{8,9},{9,10},{10,1... | collective-permute-start | bytes 196616 | tf_op jit(solution)/shard_map/ppermute | solution.py:22
  50.8 1.9 collective-permute-start.12
  50.8 4.9 %collective-permute-start.13 = (f32[1,1,32,512]{3,2,1,0:T(8,128)S(1)}, f32[1,1,32,512]{3,2,1,0:T(8,128)S(1)}, u32[]{:S(2)}, u32[]{:S(2)}) collective-permute-start(f32[1,1,32,512]{3,2,1,0:T(8,128)S(1)} %get-tuple-element.85), channel_id=1, source_target_pairs={{0,1},{1,2},{2,3},{3,4},{4,5},{5,6},{6,7},{7,0},{8,9},{9,10},{10,1... | collective-permute-start | bytes 196616 | tf_op jit(solution)/shard_map/ppermute | solution.py:22
  56.1 1.9 collective-permute-start.14
  56.2 4.9 %collective-permute-start.15 = (f32[1,1,32,512]{3,2,1,0:T(8,128)S(1)}, f32[1,1,32,512]{3,2,1,0:T(8,128)S(1)}, u32[]{:S(2)}, u32[]{:S(2)}) collective-permute-start(f32[1,1,32,512]{3,2,1,0:T(8,128)S(1)} %get-tuple-element.79), channel_id=1, source_target_pairs={{0,1},{1,2},{2,3},{3,4},{4,5},{5,6},{6,7},{7,0},{8,9},{9,10},{10,1... | collective-permute-start | bytes 196616 | tf_op jit(solution)/shard_map/ppermute | solution.py:22
  61.5 1.9 collective-permute-start.16
  61.5 4.9 %collective-permute-start.17 = (f32[1,1,32,512]{3,2,1,0:T(8,128)S(1)}, f32[1,1,32,512]{3,2,1,0:T(8,128)S(1)}, u32[]{:S(2)}, u32[]{:S(2)}) collective-permute-start(f32[1,1,32,512]{3,2,1,0:T(8,128)S(1)} %get-tuple-element.73), channel_id=1, source_target_pairs={{0,1},{1,2},{2,3},{3,4},{4,5},{5,6},{6,7},{7,0},{8,9},{9,10},{10,1... | collective-permute-start | bytes 196616 | tf_op jit(solution)/shard_map/ppermute | solution.py:22
  66.8 1.9 collective-permute-start.18
  66.8 4.9 %collective-permute-start.19 = (f32[1,1,32,512]{3,2,1,0:T(8,128)S(1)}, f32[1,1,32,512]{3,2,1,0:T(8,128)S(1)}, u32[]{:S(2)}, u32[]{:S(2)}) collective-permute-start(f32[1,1,32,512]{3,2,1,0:T(8,128)S(1)} %get-tuple-element.67), channel_id=1, source_target_pairs={{0,1},{1,2},{2,3},{3,4},{4,5},{5,6},{6,7},{7,0},{8,9},{9,10},{10,1... | collective-permute-start | bytes 196616 | tf_op jit(solution)/shard_map/ppermute | solution.py:22
  72.2 1.9 collective-permute-start.20
  72.2 4.9 %collective-permute-start.21 = (f32[1,1,32,512]{3,2,1,0:T(8,128)S(1)}, f32[1,1,32,512]{3,2,1,0:T(8,128)S(1)}, u32[]{:S(2)}, u32[]{:S(2)}) collective-permute-start(f32[1,1,32,512]{3,2,1,0:T(8,128)S(1)} %get-tuple-element.57), channel_id=1, source_target_pairs={{0,1},{1,2},{2,3},{3,4},{4,5},{5,6},{6,7},{7,0},{8,9},{9,10},{10,1... | collective-permute-start | bytes 196616 | tf_op jit(solution)/shard_map/ppermute | solution.py:22
  72.9 5.5 %copy-start.3 = (s32[16]{0:T(128)S(1)}, s32[16]{0:T(128)}, u32[]{:S(2)}) copy-start(s32[16]{0:T(128)} %param.8) | copy-start | bytes 196
  78.3 280.5 %all-gather.7.cloned.1.call-start = ((), (), s32[]{:S(2)}) async-start(), calls=%async_computation.1 | async-start | bytes 3145728 | tf_op jit(solution)/shard_map/all_gather | solution.py:165
  79.6 190.8 %copy-start.5 = (u32[256]{0:T(256)S(1)}, u32[256]{0:T(256)}, u32[]{:S(2)}) copy-start(u32[256]{0:T(256)} %constant.156) | copy-start | bytes 3076
  79.6 191.4 %copy-start.4 = (u32[256]{0:T(256)S(1)}, u32[256]{0:T(256)}, u32[]{:S(2)}) copy-start(u32[256]{0:T(256)} %constant.161) | copy-start | bytes 3076
  79.6 192.6 %copy-start.1 = (f32[4,512]{1,0:T(4,128)S(1)}, f32[4,512]{1,0:T(4,128)}, u32[]{:S(2)}) copy-start(f32[4,512]{1,0:T(4,128)} %param.6) | copy-start | bytes 24580
  79.6 192.6 %copy-start.2 = (f32[4,512]{1,0:T(4,128)S(1)}, f32[4,512]{1,0:T(4,128)}, u32[]{:S(2)}) copy-start(f32[4,512]{1,0:T(4,128)} %param.7) | copy-start | bytes 24580
Sparse Core Ops, SparseCore 0:
  78.4 182.8 all-gather.4
  270.5 58.8 all-gather.6
where the time goes:
time: 371 us; the launch traced here: 370 us
  waiting for transfers between devices  231 us (62%)
  blocking collectives  76.8 us (21%)
  other arithmetic  23.1 us (6%)
  between operations  20.7 us (6%)
  starting transfers between devices  10.6 us (3%)
  local copies, waits for them, and re-layouts  7.69 us (2%)
    all_gather x1, waiting for transfers between devices, shards(): piece = lax.all_gather(stepped[None], 'isl', axis=0, tiled=True)  182 us
    unnamed x2, blocking collectives  61.7 us
    ppermute x11, waiting for transfers between devices, extended_2(): lax.ppermute(tail, axis, [(i, (i + 1) % count) for i in range(count)])  37 us
    psum x1, blocking collectives, shards(): misfit = lax.psum(partial_value, 'sp')  15 us
    ppermute x11, waiting for transfers between devices, extended_2(): lax.ppermute(head, axis, [((i + 1) % count, i) for i in range(count)])  12.7 us
    reduce_sum x1, other arithmetic, shards(): copied = jnp.sum(jnp.where(matched, piece, 0.0), axis=0, keepdims=True)  9.07 us
  transfers between devices with their start and end apart: 24, of which 22 were waited for; matrix products, arithmetic and copies ran while one was open for 3% of the time, Pallas kernels for 0%

commit v1 on v0

--- a/solution.py
+++ b/solution.py
@@ -1,6 +1,9 @@
+import functools
 import jax
 import jax.numpy as jnp
 from jax import lax
+from jax.experimental import pallas as pl
+from jax.experimental.pallas import tpu as pltpu
 from jax.sharding import PartitionSpec as P
 
 SWEEPS = 8
@@ -98,18 +101,172 @@
     return middle + relaxation * (neighbours(padded) - 6.0 * middle - divergence) / 6.0
 
 
-def log_total(values, axis_index):
-    upper_boundary = jnp.max(values, axis=axis_index, keepdims=True)
-    return jnp.squeeze(upper_boundary, axis_index) + jnp.log(
-        jnp.sum(jnp.exp(values - upper_boundary), axis=axis_index)
-    )
+MESH = pl.DeviceIdType.MESH
+NPEER = 32
+GROUPS = ((0, 1), (1, 1), (2, 1), (3, 1))
+
+
+def place_of(flat):
+    return {"isl": flat % 16, "par": flat // 16}
+
+
+def peer_of(me, k):
+    z = (me // 4 + k // 4) % 8
+    x = (me % 4 + k % 4) % 4
+    return z * 4 + x
+
+
+def chunk_of(ref, first, count, flat):
+    row = flat // 8
+    level = pl.multiple_of((flat // 2) % 4 * 8, 8)
+    lane = pl.multiple_of(flat % 2 * 256, 256)
+    return ref.at[pl.ds(first, count), row, pl.ds(level, 8), pl.ds(lane, 256)]
+
+
+def route_kernel(anc, field, part, pick, out, logp, logi, *scratch):
+    ng = len(GROUPS)
+    held = scratch[:ng]
+    sent = scratch[ng : 2 * ng]
+    picks, parts, totals, s1, r1, s2, r2, ssem, rsem = scratch[2 * ng :]
+    isl = lax.axis_index("isl")
+    par = lax.axis_index("par")
+    sp = lax.axis_index("sp")
+    me = par * 16 + isl
+    barrier = pltpu.get_barrier_semaphore()
+
+    @pl.loop(1, NPEER)
+    def _(k):
+        pl.semaphore_signal(barrier, inc=1, device_id=place_of(peer_of(me, k)), device_id_type=MESH)
+
+    @pl.loop(1, 8)
+    def _(k):
+        pl.semaphore_signal(barrier, inc=1, device_id={"sp": (sp + k) % 8}, device_id_type=MESH)
+
+    pl.semaphore_wait(barrier, NPEER - 1 + 7)
+
+    def small(src, dst, sem, where):
+        return pltpu.make_async_remote_copy(
+            src_ref=src, dst_ref=dst, send_sem=ssem.at[sem], recv_sem=rsem.at[sem], device_id=where, device_id_type=MESH
+        )
+
+    picks[me] = pick[...]
+    parts[sp] = part[...]
+
+    @pl.loop(1, NPEER)
+    def _(k):
+        small(pick, picks.at[me], 0, place_of(peer_of(me, k))).start()
+
+    @pl.loop(1, 8)
+    def _(k):
+        small(part, parts.at[sp], 1, {"sp": (sp + k) % 8}).start()
+
+    def first_copy(g, to):
+        f0, n = GROUPS[g]
+        return pltpu.make_async_remote_copy(
+            src_ref=chunk_of(field, f0, n, to), dst_ref=held[g].at[me], send_sem=s1.at[g], recv_sem=r1.at[g],
+            device_id=place_of(to), device_id_type=MESH)
+
+    def second_copy(g, to):
+        f0, n = GROUPS[g]
+        return pltpu.make_async_remote_copy(
+            src_ref=sent[g].at[to], dst_ref=chunk_of(out, f0, n, me), send_sem=s2.at[g], recv_sem=r2.at[g],
+            device_id=place_of(to), device_id_type=MESH)
+
+    def all_of(g, s, r):
+        return pltpu.make_async_remote_copy(
+            src_ref=sent[g].at[pl.ds(0, NPEER - 1)], dst_ref=held[g].at[pl.ds(0, NPEER - 1)], send_sem=s.at[g],
+            recv_sem=r.at[g], device_id={"sp": (sp + 1) % 8}, device_id_type=MESH)
+
+    for g in range(ng):
+        f0, n = GROUPS[g]
+        held[g][me] = chunk_of(field, f0, n, me)[...]
+
+        @pl.loop(1, NPEER)
+        def _(k):
+            first_copy(g, peer_of(me, k)).start()
+
+    small(parts.at[pl.ds(0, 7)], parts.at[pl.ds(0, 7)], 1, {"sp": (sp + 1) % 8}).wait()
+    mis = parts[0]
+    for k in range(1, 8):
+        mis = mis + parts[k]
+    totals[me] = -0.5 * mis
+
+    @pl.loop(1, NPEER)
+    def _(k):
+        small(totals.at[me], totals.at[me], 2, place_of(peer_of(me, k))).start()
+
+    small(picks.at[pl.ds(0, NPEER - 1)], picks.at[pl.ds(0, NPEER - 1)], 0, {"sp": (sp + 1) % 8}).wait()
+
+    for g in range(ng):
+        f0, n = GROUPS[g]
+        all_of(g, s1, r1).wait_recv()
+
+        @pl.loop(0, NPEER)
+        def _(d):
+            src = anc[d % 16]
+            choose = jnp.broadcast_to(picks[d][None], (n, 8, 128))
+            for h in range(2):
+                lo = held[g][src, :, :, h * 128 : (h + 1) * 128]
+                hi = held[g][src + 16, :, :, h * 128 : (h + 1) * 128]
+                sent[g][d, :, :, h * 128 : (h + 1) * 128] = jnp.where(choose < 0.5, lo, hi)
+
+        @pl.loop(1, NPEER)
+        def _(k):
+            second_copy(g, peer_of(me, k)).start()
+
+        chunk_of(out, f0, n, me)[...] = sent[g][me]
+
+    small(totals.at[pl.ds(0, NPEER - 1)], totals.at[pl.ds(0, NPEER - 1)], 2, {"sp": (sp + 1) % 8}).wait()
+    a = totals[0:16]
+    b = totals[16:32]
+    top = jnp.maximum(a, b)
+    isle = top + jnp.log(jnp.exp(a - top) + jnp.exp(b - top))
+    peak = jnp.max(isle, axis=0)
+    whole = peak + jnp.log(jnp.sum(jnp.exp(isle - peak[None]), axis=0))
+    a1 = totals[isl]
+    b1 = totals[isl + 16]
+    top1 = jnp.maximum(a1, b1)
+    mine = top1 + jnp.log(jnp.exp(a1 - top1) + jnp.exp(b1 - top1))
+    logp[...] = totals[me] - mine
+    logi[...] = mine - whole
+
+    for g in range(ng):
+        all_of(g, s1, r1).wait_send()
+        all_of(g, s2, r2).wait()
+
+
+def route(anc, field, part, pick):
+    vmem = pl.BlockSpec(memory_space=pltpu.VMEM)
+    smem = pl.BlockSpec(memory_space=pltpu.SMEM)
+    bufs = [pltpu.VMEM((NPEER, n, 8, 256), jnp.float32) for _, n in GROUPS]
+    ng = len(GROUPS)
+    return pl.pallas_call(
+        route_kernel,
+        out_shape=(
+            jax.ShapeDtypeStruct(field.shape, jnp.float32),
+            jax.ShapeDtypeStruct((1, 128), jnp.float32),
+            jax.ShapeDtypeStruct((1, 128), jnp.float32),
+        ),
+        in_specs=[smem, vmem, vmem, vmem],
+        out_specs=(vmem, vmem, vmem),
+        scratch_shapes=bufs + bufs + [
+            pltpu.VMEM((NPEER, 1, 128), jnp.float32),
+            pltpu.VMEM((8, 1, 128), jnp.float32),
+            pltpu.VMEM((NPEER, 1, 128), jnp.float32),
+            pltpu.SemaphoreType.DMA((ng,)),
+            pltpu.SemaphoreType.DMA((ng,)),
+            pltpu.SemaphoreType.DMA((ng,)),
+            pltpu.SemaphoreType.DMA((ng,)),
+            pltpu.SemaphoreType.DMA((3,)),
+            pltpu.SemaphoreType.DMA((3,)),
+        ],
+        compiler_params=pltpu.CompilerParams(collective_id=0, has_side_effects=True),
+    )(anc, field, part, pick)
 
 
 def shards(ensemble, observations, obs_precision, island_ancestor, particle_ancestor):
     model_state = ensemble[0]
     rows_east = model_state.shape[2]
-    island_now = lax.axis_index("isl")
-    source_island = island_ancestor[island_now]
     picks = particle_ancestor[0]
     zonal = model_state[:, 0]
     merid = model_state[:, 1]
@@ -150,21 +307,10 @@
     ramp = 1.0 + positions * (2.0 / (nx_total - 1))
     scale = obs_precision * ramp[:, None]
     partial_value = jnp.sum((upper_boundary - observations) ** 2 * scale, axis=(1, 2))
-    misfit = lax.psum(partial_value, "sp")
-    log_weight = -0.5 * misfit
-    island_weights = lax.all_gather(log_weight, "par", axis=0, tiled=True)
-    island_total = log_total(island_weights, 0)
-    particle_out = log_weight - island_total
-    totals = lax.all_gather(island_total[None], "isl", axis=0, tiled=True)
-    island_out = island_total - log_total(totals, 0)
-    particle_out, island_out = (particle_out, island_out)
-    piece = lax.all_gather(stepped[None], "isl", axis=0, tiled=True)
-    labels = jnp.arange(piece.shape[0], dtype=jnp.int32)
-    matched = (labels == source_island)[:, None, None, None, None, None]
-    copied = jnp.sum(jnp.where(matched, piece, 0.0), axis=0, keepdims=True)
-    complete_island_state = lax.all_gather(copied, "par", axis=1, tiled=True)
-    result = jnp.take(complete_island_state[0], picks, axis=0)
-    return (result[None], particle_out[None], island_out[None])
+    part = jnp.broadcast_to(partial_value[:, None], (1, 128))
+    pick = jnp.broadcast_to(picks[:, None].astype(jnp.float32), (1, 128))
+    out, logp, logi = route(island_ancestor, stepped[0], part, pick)
+    return (out[None, None], logp[:, :1], logi[0, :1])
 
 
 def solution(mesh):

time: 371 us -> 140 us (0.38)
  the two profiles are of different devices: /device:TPU:128 before, /device:TPU:25 now
where the time goes in v1:
time: 140 us; the launch traced here: 137 us
  Pallas kernels  59.6 us (43%)
  waiting for transfers between devices  48.2 us (34%)
  starting transfers between devices  10.6 us (8%)
  local copies, waits for them, and re-layouts  9.39 us (7%)
  other arithmetic  5.99 us (4%)
  between operations  3.43 us (2%)
    pallas_call x1, Pallas kernels, route(): pl.pallas_call(route_kernel, out_shape=(jax.ShapeDtypeStruct(field.shape,...  59.6 us
    ppermute x11, waiting for transfers between devices, extended_2(): lax.ppermute(head, axis, [((i + 1) % count, i) for i in range(count)])  41.5 us
    ppermute x11, waiting for transfers between devices, extended_2(): lax.ppermute(tail, axis, [(i, (i + 1) % count) for i in range(count)])  6.64 us
    ppermute x11, starting transfers between devices, extended_2(): lax.ppermute(tail, axis, [(i, (i + 1) % count) for i in range(count)])  5.41 us
    ppermute x11, starting transfers between devices, extended_2(): lax.ppermute(head, axis, [((i + 1) % count, i) for i in range(count)])  5.16 us
  transfers between devices with their start and end apart: 22, of which 20 were waited for; matrix products, arithmetic and copies ran while one was open for 2% of the time, Pallas kernels for 0%

profile of v1, /device:TPU:25, one launch (start us, length us, event | category | flops | bytes accessed | tf_op | source)
XLA Modules:
  0.0 137.2 jit_solution(6788910908131581328)
XLA Ops:
  0.6 1.4 %fusion.177 = (f32[1,4,2,32,512]{4,3,2,1,0:T(8,128)S(1)}, f32[1,4,2,32,512]{4,3,2,1,0:T(8,128)S(1)}) fusion(f32[1,4,4,32,512]{4,3,2,1,0:T(8,128)} %bitcast.67), kind=kLoop, calls=%fused_computation.271 | loop fusion | bytes 2097152 | tf_op jit(solution)/shard_map/slice | solution.py:22
  2.0 0.7 collective-permute-start.1
  2.7 2.3 %collective-permute-start = (f32[1,4,2,32,512]{4,3,2,1,0:T(8,128)S(1)}, f32[1,4,2,32,512]{4,3,2,1,0:T(8,128)S(1)}, u32[]{:S(2)}, u32[]{:S(2)}) collective-permute-start(f32[1,4,2,32,512]{4,3,2,1,0:T(8,128)S(1)} %get-tuple-element.15), channel_id=1, source_target_pairs={{0,1},{1,2},{2,3},{3,4},{4,5},{5,6},{6,7},{7,0},{8,9},{9,10},{10,1... | collective-permute-start | bytes 1572872 | tf_op jit(solution)/shard_map/ppermute | solution.py:25
  5.7 6.2 %collective-permute-done.1 = f32[1,4,2,32,512]{4,3,2,1,0:T(8,128)S(1)} collective-permute-done((f32[1,4,2,32,512]{4,3,2,1,0:T(8,128)S(1)}, f32[1,4,2,32,512]{4,3,2,1,0:T(8,128)S(1)}, u32[]{:S(2)}, u32[]{:S(2)}) %collective-permute-start.1) | collective-permute-done | bytes 524320 | tf_op jit(solution)/shard_map/ppermute | solution.py:27
  14.8 3.0 %collective-permute-start.3 = (f32[1,1,32,512]{3,2,1,0:T(8,128)S(1)}, f32[1,1,32,512]{3,2,1,0:T(8,128)S(1)}, u32[]{:S(2)}, u32[]{:S(2)}) collective-permute-start(f32[1,1,32,512]{3,2,1,0:T(8,128)S(1)} %get-tuple-element.106), channel_id=1, source_target_pairs={{0,1},{1,2},{2,3},{3,4},{4,5},{5,6},{6,7},{7,0},{8,9},{9,10},{10,1... | collective-permute-start | bytes 196616 | tf_op jit(solution)/shard_map/ppermute | solution.py:25
  19.0 0.7 fusion.175
  19.7 3.0 %collective-permute-done.2 = f32[1,1,32,512]{3,2,1,0:T(8,128)S(1)} collective-permute-done((f32[1,1,32,512]{3,2,1,0:T(8,128)S(1)}, f32[1,1,32,512]{3,2,1,0:T(8,128)S(1)}, u32[]{:S(2)}, u32[]{:S(2)}) %collective-permute-start.2) | collective-permute-done | bytes 65568 | tf_op jit(solution)/shard_map/ppermute | solution.py:27
  23.1 0.5 collective-permute-start.4
  23.6 0.7 collective-permute-done.5
  24.4 3.6 %collective-permute-done.4 = f32[1,1,32,512]{3,2,1,0:T(8,128)S(1)} collective-permute-done((f32[1,1,32,512]{3,2,1,0:T(8,128)S(1)}, f32[1,1,32,512]{3,2,1,0:T(8,128)S(1)}, u32[]{:S(2)}, u32[]{:S(2)}) %collective-permute-start.4) | collective-permute-done | bytes 65568 | tf_op jit(solution)/shard_map/ppermute | solution.py:27
  29.0 0.7 collective-permute-done.7
  29.7 3.6 %collective-permute-done.6 = f32[1,1,32,512]{3,2,1,0:T(8,128)S(1)} collective-permute-done((f32[1,1,32,512]{3,2,1,0:T(8,128)S(1)}, f32[1,1,32,512]{3,2,1,0:T(8,128)S(1)}, u32[]{:S(2)}, u32[]{:S(2)}) %collective-permute-start.6) | collective-permute-done | bytes 65568 | tf_op jit(solution)/shard_map/ppermute | solution.py:27
  34.3 0.7 collective-permute-done.9
  35.0 3.6 %collective-permute-done.8 = f32[1,1,32,512]{3,2,1,0:T(8,128)S(1)} collective-permute-done((f32[1,1,32,512]{3,2,1,0:T(8,128)S(1)}, f32[1,1,32,512]{3,2,1,0:T(8,128)S(1)}, u32[]{:S(2)}, u32[]{:S(2)}) %collective-permute-start.8) | collective-permute-done | bytes 65568 | tf_op jit(solution)/shard_map/ppermute | solution.py:27
  39.6 0.7 collective-permute-done.11
  40.4 3.6 %collective-permute-done.10 = f32[1,1,32,512]{3,2,1,0:T(8,128)S(1)} collective-permute-done((f32[1,1,32,512]{3,2,1,0:T(8,128)S(1)}, f32[1,1,32,512]{3,2,1,0:T(8,128)S(1)}, u32[]{:S(2)}, u32[]{:S(2)}) %collective-permute-start.10) | collective-permute-done | bytes 65568 | tf_op jit(solution)/shard_map/ppermute | solution.py:27
  45.0 0.7 collective-permute-done.13
  45.7 3.6 %collective-permute-done.12 = f32[1,1,32,512]{3,2,1,0:T(8,128)S(1)} collective-permute-done((f32[1,1,32,512]{3,2,1,0:T(8,128)S(1)}, f32[1,1,32,512]{3,2,1,0:T(8,128)S(1)}, u32[]{:S(2)}, u32[]{:S(2)}) %collective-permute-start.12) | collective-permute-done | bytes 65568 | tf_op jit(solution)/shard_map/ppermute | solution.py:27
  50.3 0.7 collective-permute-done.15
  51.0 3.6 %collective-permute-done.14 = f32[1,1,32,512]{3,2,1,0:T(8,128)S(1)} collective-permute-done((f32[1,1,32,512]{3,2,1,0:T(8,128)S(1)}, f32[1,1,32,512]{3,2,1,0:T(8,128)S(1)}, u32[]{:S(2)}, u32[]{:S(2)}) %collective-permute-start.14) | collective-permute-done | bytes 65568 | tf_op jit(solution)/shard_map/ppermute | solution.py:27
  55.0 0.5 collective-permute-start.16
  55.6 0.7 collective-permute-done.17
  56.4 3.6 %collective-permute-done.16 = f32[1,1,32,512]{3,2,1,0:T(8,128)S(1)} collective-permute-done((f32[1,1,32,512]{3,2,1,0:T(8,128)S(1)}, f32[1,1,32,512]{3,2,1,0:T(8,128)S(1)}, u32[]{:S(2)}, u32[]{:S(2)}) %collective-permute-start.16) | collective-permute-done | bytes 65568 | tf_op jit(solution)/shard_map/ppermute | solution.py:27
  61.0 0.7 collective-permute-done.19
  61.7 3.6 %collective-permute-done.18 = f32[1,1,32,512]{3,2,1,0:T(8,128)S(1)} collective-permute-done((f32[1,1,32,512]{3,2,1,0:T(8,128)S(1)}, f32[1,1,32,512]{3,2,1,0:T(8,128)S(1)}, u32[]{:S(2)}, u32[]{:S(2)}) %collective-permute-start.18) | collective-permute-done | bytes 65568 | tf_op jit(solution)/shard_map/ppermute | solution.py:27
  66.4 0.7 collective-permute-done.21
  67.1 3.6 %collective-permute-done.20 = f32[1,1,32,512]{3,2,1,0:T(8,128)S(1)} collective-permute-done((f32[1,1,32,512]{3,2,1,0:T(8,128)S(1)}, f32[1,1,32,512]{3,2,1,0:T(8,128)S(1)}, u32[]{:S(2)}, u32[]{:S(2)}) %collective-permute-start.20) | collective-permute-done | bytes 65568 | tf_op jit(solution)/shard_map/ppermute | solution.py:27
  70.8 1.0 maximum_bitcast_fusion.field
  71.8 1.2 broadcast_in_dim.8.part
  73.0 0.5 broadcast_in_dim.10.pick
  73.5 59.6 %shard_map.76 = (f32[4,4,32,512]{3,2,1,0:T(8,128)}, f32[1,128]{1,0:T(1,128)}, f32[1,128]{1,0:T(1,128)}) custom-call(s32[16]{0:T(128)} %anc.1, f32[4,4,32,512]{3,2,1,0:T(8,128)} %maximum_bitcast_fusion.field, f32[1,128]{1,0:T(1,128)} %broadcast_in_dim.8.part, f32[1,128]{1,0:T(1,128)} %broadcast_in_dim.10.pick), custom_call_target="tpu_custom_call" | custom-call | tf_op jit(solution)/shard_map/pallas_call | solution.py:243
  133.2 2.3 %copy.14 = f32[1,1,4,4,32,512]{5,4,3,2,1,0:T(8,128)} copy(f32[1,1,4,4,32,512]{5,4,3,2,1,0:T(8,128)} %bitcast.74) | data formatting | bytes 2097152
  (90 shorter events, 12.0 us)
Async XLA Ops:
  0.6 11.2 %copy-start = (f32[1,1,4,4,32,512]{5,4,3,2,1,0:T(8,128)S(1)}, f32[1,1,4,4,32,512]{5,4,3,2,1,0:T(8,128)}, u32[]{:S(2)}) copy-start(f32[1,1,4,4,32,512]{5,4,3,2,1,0:T(8,128)} %param.5) | copy-start | bytes 3145732
  2.0 9.8 %collective-permute-start.1 = (f32[1,4,2,32,512]{4,3,2,1,0:T(8,128)S(1)}, f32[1,4,2,32,512]{4,3,2,1,0:T(8,128)S(1)}, u32[]{:S(2)}, u32[]{:S(2)}) collective-permute-start(f32[1,4,2,32,512]{4,3,2,1,0:T(8,128)S(1)} %get-tuple-element.16), channel_id=1, source_target_pairs={{1,0},{2,1},{3,2},{4,3},{5,4},{6,5},{7,6},{0,7},{9,8},{10,9},{11,1... | collective-permute-start | bytes 1572872 | tf_op jit(solution)/shard_map/ppermute | solution.py:27
  2.7 9.1 %collective-permute-start = (f32[1,4,2,32,512]{4,3,2,1,0:T(8,128)S(1)}, f32[1,4,2,32,512]{4,3,2,1,0:T(8,128)S(1)}, u32[]{:S(2)}, u32[]{:S(2)}) collective-permute-start(f32[1,4,2,32,512]{4,3,2,1,0:T(8,128)S(1)} %get-tuple-element.15), channel_id=1, source_target_pairs={{0,1},{1,2},{2,3},{3,4},{4,5},{5,6},{6,7},{7,0},{8,9},{9,10},{10,1... | collective-permute-start | bytes 1572872 | tf_op jit(solution)/shard_map/ppermute | solution.py:25
  14.8 4.8 %collective-permute-start.3 = (f32[1,1,32,512]{3,2,1,0:T(8,128)S(1)}, f32[1,1,32,512]{3,2,1,0:T(8,128)S(1)}, u32[]{:S(2)}, u32[]{:S(2)}) collective-permute-start(f32[1,1,32,512]{3,2,1,0:T(8,128)S(1)} %get-tuple-element.106), channel_id=1, source_target_pairs={{0,1},{1,2},{2,3},{3,4},{4,5},{5,6},{6,7},{7,0},{8,9},{9,10},{10,1... | collective-permute-start | bytes 196616 | tf_op jit(solution)/shard_map/ppermute | solution.py:25
  17.8 4.9 %collective-permute-start.2 = (f32[1,1,32,512]{3,2,1,0:T(8,128)S(1)}, f32[1,1,32,512]{3,2,1,0:T(8,128)S(1)}, u32[]{:S(2)}, u32[]{:S(2)}) collective-permute-start(f32[1,1,32,512]{3,2,1,0:T(8,128)S(1)} %get-tuple-element.105), channel_id=1, source_target_pairs={{1,0},{2,1},{3,2},{4,3},{5,4},{6,5},{7,6},{0,7},{9,8},{10,9},{11,1... | collective-permute-start | bytes 196616 | tf_op jit(solution)/shard_map/ppermute | solution.py:27
  18.3 0.7 copy-start.1
  18.3 0.7 copy-start.2
  23.0 1.4 collective-permute-start.5
  23.1 4.9 %collective-permute-start.4 = (f32[1,1,32,512]{3,2,1,0:T(8,128)S(1)}, f32[1,1,32,512]{3,2,1,0:T(8,128)S(1)}, u32[]{:S(2)}, u32[]{:S(2)}) collective-permute-start(f32[1,1,32,512]{3,2,1,0:T(8,128)S(1)} %get-tuple-element.103), channel_id=1, source_target_pairs={{1,0},{2,1},{3,2},{4,3},{5,4},{6,5},{7,6},{0,7},{9,8},{10,9},{11,1... | collective-permute-start | bytes 196616 | tf_op jit(solution)/shard_map/ppermute | solution.py:27
  28.4 1.4 collective-permute-start.7
  28.4 4.9 %collective-permute-start.6 = (f32[1,1,32,512]{3,2,1,0:T(8,128)S(1)}, f32[1,1,32,512]{3,2,1,0:T(8,128)S(1)}, u32[]{:S(2)}, u32[]{:S(2)}) collective-permute-start(f32[1,1,32,512]{3,2,1,0:T(8,128)S(1)} %get-tuple-element.97), channel_id=1, source_target_pairs={{1,0},{2,1},{3,2},{4,3},{5,4},{6,5},{7,6},{0,7},{9,8},{10,9},{11,1... | collective-permute-start | bytes 196616 | tf_op jit(solution)/shard_map/ppermute | solution.py:27
  33.7 1.4 collective-permute-start.9
  33.7 4.9 %collective-permute-start.8 = (f32[1,1,32,512]{3,2,1,0:T(8,128)S(1)}, f32[1,1,32,512]{3,2,1,0:T(8,128)S(1)}, u32[]{:S(2)}, u32[]{:S(2)}) collective-permute-start(f32[1,1,32,512]{3,2,1,0:T(8,128)S(1)} %get-tuple-element.91), channel_id=1, source_target_pairs={{1,0},{2,1},{3,2},{4,3},{5,4},{6,5},{7,6},{0,7},{9,8},{10,9},{11,1... | collective-permute-start | bytes 196616 | tf_op jit(solution)/shard_map/ppermute | solution.py:27
  39.0 1.4 collective-permute-start.11
  39.0 4.9 %collective-permute-start.10 = (f32[1,1,32,512]{3,2,1,0:T(8,128)S(1)}, f32[1,1,32,512]{3,2,1,0:T(8,128)S(1)}, u32[]{:S(2)}, u32[]{:S(2)}) collective-permute-start(f32[1,1,32,512]{3,2,1,0:T(8,128)S(1)} %get-tuple-element.85), channel_id=1, source_target_pairs={{1,0},{2,1},{3,2},{4,3},{5,4},{6,5},{7,6},{0,7},{9,8},{10,9},{11,1... | collective-permute-start | bytes 196616 | tf_op jit(solution)/shard_map/ppermute | solution.py:27
  44.4 1.4 collective-permute-start.13
  44.4 4.9 %collective-permute-start.12 = (f32[1,1,32,512]{3,2,1,0:T(8,128)S(1)}, f32[1,1,32,512]{3,2,1,0:T(8,128)S(1)}, u32[]{:S(2)}, u32[]{:S(2)}) collective-permute-start(f32[1,1,32,512]{3,2,1,0:T(8,128)S(1)} %get-tuple-element.79), channel_id=1, source_target_pairs={{1,0},{2,1},{3,2},{4,3},{5,4},{6,5},{7,6},{0,7},{9,8},{10,9},{11,1... | collective-permute-start | bytes 196616 | tf_op jit(solution)/shard_map/ppermute | solution.py:27
  49.7 1.4 collective-permute-start.15
  49.7 4.9 %collective-permute-start.14 = (f32[1,1,32,512]{3,2,1,0:T(8,128)S(1)}, f32[1,1,32,512]{3,2,1,0:T(8,128)S(1)}, u32[]{:S(2)}, u32[]{:S(2)}) collective-permute-start(f32[1,1,32,512]{3,2,1,0:T(8,128)S(1)} %get-tuple-element.73), channel_id=1, source_target_pairs={{1,0},{2,1},{3,2},{4,3},{5,4},{6,5},{7,6},{0,7},{9,8},{10,9},{11,1... | collective-permute-start | bytes 196616 | tf_op jit(solution)/shard_map/ppermute | solution.py:27
  55.0 1.4 collective-permute-start.17
  55.0 4.9 %collective-permute-start.16 = (f32[1,1,32,512]{3,2,1,0:T(8,128)S(1)}, f32[1,1,32,512]{3,2,1,0:T(8,128)S(1)}, u32[]{:S(2)}, u32[]{:S(2)}) collective-permute-start(f32[1,1,32,512]{3,2,1,0:T(8,128)S(1)} %get-tuple-element.67), channel_id=1, source_target_pairs={{1,0},{2,1},{3,2},{4,3},{5,4},{6,5},{7,6},{0,7},{9,8},{10,9},{11,1... | collective-permute-start | bytes 196616 | tf_op jit(solution)/shard_map/ppermute | solution.py:27
  60.3 1.4 collective-permute-start.19
  60.4 4.9 %collective-permute-start.18 = (f32[1,1,32,512]{3,2,1,0:T(8,128)S(1)}, f32[1,1,32,512]{3,2,1,0:T(8,128)S(1)}, u32[]{:S(2)}, u32[]{:S(2)}) collective-permute-start(f32[1,1,32,512]{3,2,1,0:T(8,128)S(1)} %get-tuple-element.61), channel_id=1, source_target_pairs={{1,0},{2,1},{3,2},{4,3},{5,4},{6,5},{7,6},{0,7},{9,8},{10,9},{11,1... | collective-permute-start | bytes 196616 | tf_op jit(solution)/shard_map/ppermute | solution.py:27
  65.8 1.4 collective-permute-start.21
  65.8 4.9 %collective-permute-start.20 = (f32[1,1,32,512]{3,2,1,0:T(8,128)S(1)}, f32[1,1,32,512]{3,2,1,0:T(8,128)S(1)}, u32[]{:S(2)}, u32[]{:S(2)}) collective-permute-start(f32[1,1,32,512]{3,2,1,0:T(8,128)S(1)} %get-tuple-element.51), channel_id=1, source_target_pairs={{1,0},{2,1},{3,2},{4,3},{5,4},{6,5},{7,6},{0,7},{9,8},{10,9},{11,1... | collective-permute-start | bytes 196616 | tf_op jit(solution)/shard_map/ppermute | solution.py:27
  133.2 2.3 %copy-start.4 = (f32[1,128]{1,0:T(1,128)S(1)}, f32[1,128]{1,0:T(1,128)}, u32[]{:S(2)}) copy-start(f32[1,128]{1,0:T(1,128)} %get-tuple-element.7) | copy-start | bytes 1540
  133.2 2.8 %copy-start.3 = (f32[1,128]{1,0:T(1,128)S(1)}, f32[1,128]{1,0:T(1,128)}, u32[]{:S(2)}) copy-start(f32[1,128]{1,0:T(1,128)} %get-tuple-element.8) | copy-start | bytes 1540

commit v2 on v1

v2 whole, which is shorter than its diff:
```python
import jax
import jax.numpy as jnp
from jax import lax
from jax.experimental import pallas as pl
from jax.experimental.pallas import tpu as pltpu
from jax.sharding import PartitionSpec as P

MESH = pl.DeviceIdType.MESH
NPEER = 32
ORDER = (3, 0, 1, 2)
STEP = 0.2
VISC = 0.05
STRAT = 1.0
RELAX = 0.8
Z0 = 8
NZ = 32
LANES = 512


def place_of(flat):
    return {"isl": flat % 16, "par": flat // 16}


def peer_of(me, k):
    z = (me // 4 + k // 4) % 8
    x = (me % 4 + k % 4) % 4
    return z * 4 + x


def chunk_of(ref, flat):
    row = flat // 8
    level = pl.multiple_of((flat // 2) % 4 * 8, 8)
    lane = pl.multiple_of(flat % 2 * 256, 256)
    return ref.at[row, pl.ds(level, 8), pl.ds(lane, 256)]


def north(q, k):
    return pltpu.roll(q, k % LANES, 1)


def pad_rows(ref, rows):
    zero = jnp.zeros((8, LANES), jnp.float32)

    @pl.loop(0, rows)
    def _(r):
        ref[r, 0:Z0, :] = zero
        ref[r, Z0 + NZ : Z0 + NZ + 8, :] = zero


def kernel(
    anc, pick, obs, prec, ens, out, logp, logi,
    xu, xv, xw, xb, su, sv, sw, dv, pa, pb, p3, p6, fore,
    h0, h1, h2, h3, g0, g1, g2, g3, picks, parts, totals,
    lsem, hs, hr, s1, r1, s2, r2, ssem, rsem,
):
    held = (h0, h1, h2, h3)
    sent = (g0, g1, g2, g3)
    isl = lax.axis_index("isl")
    par = lax.axis_index("par")
    sp = lax.axis_index("sp")
    me = par * 16 + isl
    after = {"sp": (sp + 1) % 8}
    before = {"sp": (sp + 7) % 8}
    fields = (xu, xv, xw, xb)
    barrier = pltpu.get_barrier_semaphore()

    @pl.loop(1, NPEER)
    def _(k):
        pl.semaphore_signal(barrier, inc=1, device_id=place_of(peer_of(me, k)), device_id_type=MESH)

    @pl.loop(1, 8)
    def _(k):
        pl.semaphore_signal(barrier, inc=1, device_id={"sp": (sp + k) % 8}, device_id_type=MESH)

    loads = [
        pltpu.make_async_copy(ens.at[f], fields[f].at[3:7, Z0 : Z0 + NZ, :], lsem.at[f]) for f in range(4)
    ]
    for load in loads:
        load.start()

    def remote(src, dst, ss, rs, where):
        return pltpu.make_async_remote_copy(
            src_ref=src, dst_ref=dst, send_sem=ss, recv_sem=rs, device_id=where, device_id_type=MESH
        )

    def small(src, dst, sem, where):
        return remote(src, dst, ssem.at[sem], rsem.at[sem], where)

    pad_rows(xu, 10)
    pad_rows(xv, 10)
    pad_rows(xw, 10)
    pad_rows(xb, 10)
    pad_rows(sw, 4)
    pad_rows(dv, 10)
    pad_rows(pa, 8)
    pad_rows(pb, 6)
    pad_rows(p3, 10)
    pad_rows(p6, 10)
    picks[me] = jnp.full((1, 128), pick[0, 0], jnp.int32).astype(jnp.float32)

    pl.semaphore_wait(barrier, NPEER - 1 + 7)

    edges = []
    for f in range(4):
        w = 3 if f == 0 else 2
        to_after = remote(
            ens.at[f, 4 - w : 4], fields[f].at[3 - w : 3, Z0 : Z0 + NZ, :], hs.at[f, 0], hr.at[f, 0], after
        )
        to_before = remote(
            ens.at[f, 0:w], fields[f].at[7 : 7 + w, Z0 : Z0 + NZ, :], hs.at[f, 1], hr.at[f, 1], before
        )
        edges += [to_after, to_before]
    for edge in edges:
        edge.start()

    @pl.loop(1, NPEER)
    def _(k):
        small(picks.at[me], picks.at[me], 0, place_of(peer_of(me, k))).start()

    for load in loads:
        load.wait()
    for edge in edges:
        edge.wait()

    def tendency(q, r, zb, u, v, w):
        s = Z0 + 8 * zb
        c = q[r, s : s + 8, :]
        xp = q[r + 1, s : s + 8, :]
        xm = q[r - 1, s : s + 8, :]
        xpp = q[r + 2, s : s + 8, :]
        xmm = q[r - 2, s : s + 8, :]
        zp = q[r, s + 1 : s + 9, :]
        zm = q[r, s - 1 : s + 7, :]
        zpp = q[r, s + 2 : s + 10, :]
        zmm = q[r, s - 2 : s + 6, :]
        yp = north(c, -1)
        ym = north(c, 1)
        ypp = north(c, -2)
        ymm = north(c, 2)
        lap = (xp + xm) + (yp + ym) + (zp + zm) - 6.0 * c
        adv = (
            u * (8.0 * (xp - xm) - (xpp - xmm))
            + v * (8.0 * (yp - ym) - (ypp - ymm))
            + w * (8.0 * (zp - zm) - (zpp - zmm))
        )
        return c, (STEP * VISC) * lap - adv

    def winds(r, zb):
        s = Z0 + 8 * zb
        return tuple(q[r, s : s + 8, :] * (STEP / 12.0) for q in (xu, xv, xw))

    @pl.loop(0, 4)
    def _(i):
        r = i + 3
        for zb in range(4):
            s = 8 * zb
            u, v, w = winds(r, zb)
            c, g = tendency(xb, r, zb, u, v, w)
            flow = xw[r, Z0 + s : Z0 + s + 8, :]
            fore[3, i, s : s + 8, :] = c + g - (STEP * STRAT) * flow

    acc = jnp.zeros((1, LANES), jnp.float32)
    for i in range(4):
        gap = fore[3, i, NZ - 1 : NZ, :] - obs[i : i + 1, :]
        ramp = 1.0 + (sp * 4 + i).astype(jnp.float32) * (2.0 / 31.0)
        acc = acc + gap * gap * (prec[i : i + 1, :] * ramp)
    parts[sp] = jnp.broadcast_to(jnp.sum(acc, axis=1, keepdims=True), (1, 128))

    def first_copy(g, to):
        return remote(chunk_of(fore.at[g], to), held[g].at[me], s1.at[g], r1.at[g], place_of(to))

    def second_copy(g, to):
        return remote(sent[g].at[to], chunk_of(out.at[g], me), s2.at[g], r2.at[g], place_of(to))

    def all_of(g, s, r):
        return remote(
            sent[g].at[pl.ds(0, NPEER - 1)], held[g].at[pl.ds(0, NPEER - 1)], s.at[g], r.at[g], after
        )

    def start_first(g):
        held[g][me] = chunk_of(fore.at[g], me)[...]

        @pl.loop(1, NPEER)
        def _(k):
            first_copy(g, peer_of(me, k)).start()

    def start_second(g):
        all_of(g, s1, r1).wait_recv()

        @pl.loop(0, NPEER)
        def _(d):
            src = anc[d % 16]
            choose = jnp.broadcast_to(picks[d], (8, 128)) < 0.5
            for h in range(2):
                lo = held[g][src, :, h * 128 : (h + 1) * 128]
                hi = held[g][src + 16, :, h * 128 : (h + 1) * 128]
                sent[g][d, :, h * 128 : (h + 1) * 128] = jnp.where(choose, lo, hi)

        @pl.loop(1, NPEER)
        def _(k):
            second_copy(g, peer_of(me, k)).start()

        chunk_of(out.at[g], me)[...] = sent[g][me]

    start_first(3)

    @pl.loop(1, 8)
    def _(k):
        small(parts.at[sp], parts.at[sp], 1, {"sp": (sp + k) % 8}).start()

    @pl.loop(0, 6)
    def _(i):
        r = i + 2
        for zb in range(4):
            s = 8 * zb
            u, v, w = winds(r, zb)
            c, g = tendency(xu, r, zb, u, v, w)
            su[i, s : s + 8, :] = c + g

    @pl.loop(0, 4)
    def _(i):
        r = i + 3
        for zb in range(4):
            s = 8 * zb
            u, v, w = winds(r, zb)
            c, g = tendency(xv, r, zb, u, v, w)
            star = c + g
            sv[i, s : s + 8, :] = star
            dv[r, Z0 + s : Z0 + s + 8, :] = 0.5 * (north(star, -1) - north(star, 1))
            c, g = tendency(xw, r, zb, u, v, w)
            sw[i, Z0 + s : Z0 + s + 8, :] = c + g + STEP * xb[r, Z0 + s : Z0 + s + 8, :]

    @pl.loop(0, 4)
    def _(i):
        for zb in range(4):
            s = 8 * zb
            t = Z0 + s
            dx = 0.5 * (su[i + 2, s : s + 8, :] - su[i, s : s + 8, :])
            dz = 0.5 * (sw[i, t + 1 : t + 9, :] - sw[i, t - 1 : t + 7, :])
            dv[i + 3, t : t + 8, :] = dx + dv[i + 3, t : t + 8, :] + dz

    def exchange(buf, e):
        copies = (
            remote(buf.at[4:7, Z0 : Z0 + NZ, :], buf.at[0:3, Z0 : Z0 + NZ, :], hs.at[e, 0], hr.at[e, 0], after),
            remote(buf.at[3:6, Z0 : Z0 + NZ, :], buf.at[7:10, Z0 : Z0 + NZ, :], hs.at[e, 1], hr.at[e, 1], before),
        )
        for copy in copies:
            copy.start()
        return copies

    def finish(copies):
        for copy in copies:
            copy.wait()

    def sweep(src, dst, count, dst0, div0, first=False):
        @pl.loop(0, count)
        def _(i):
            for zb in range(4):
                t = Z0 + 8 * zb
                c = src[i + 1, t : t + 8, :]
                near = (
                    (src[i + 2, t : t + 8, :] + src[i, t : t + 8, :])
                    + (north(c, 1) + north(c, -1))
                    + (src[i + 1, t + 1 : t + 9, :] + src[i + 1, t - 1 : t + 7, :])
                )
                if first:
                    k = -RELAX / 6.0
                    val = (k * (1.0 - RELAX) - RELAX / 6.0) * c + (k * RELAX / 6.0) * near
                else:
                    d = dv[i + div0, t : t + 8, :]
                    val = (1.0 - RELAX) * c + (RELAX / 6.0) * (near - d)
                dst[i + dst0, t : t + 8, :] = val

    finish(exchange(dv, 4))
    sweep(dv, pa, 8, 0, 1, first=True)
    sweep(pa, pb, 6, 0, 2)
    sweep(pb, p3, 4, 3, 3)
    moving = exchange(p3, 5)

    small(parts.at[pl.ds(0, 7)], parts.at[pl.ds(0, 7)], 1, after).wait()
    mis = parts[0]
    for k in range(1, 8):
        mis = mis + parts[k]
    totals[me] = -0.5 * mis

    @pl.loop(1, NPEER)
    def _(k):
        small(totals.at[me], totals.at[me], 2, place_of(peer_of(me, k))).start()

    finish(moving)
    sweep(p3, pa, 8, 0, 1)
    sweep(pa, pb, 6, 0, 2)
    sweep(pb, p6, 4, 3, 3)
    moving = exchange(p6, 6)

    small(picks.at[pl.ds(0, NPEER - 1)], picks.at[pl.ds(0, NPEER - 1)], 0, after).wait()
    start_second(3)

    finish(moving)
    sweep(p6, pa, 8, 0, 1)
    sweep(pa, pb, 6, 0, 2)

    @pl.loop(0, 4)
    def _(i):
        for zb in range(4):
            s = 8 * zb
            t = Z0 + s
            fore[0, i, s : s + 8, :] = su[i + 1, s : s + 8, :] - 0.5 * (
                pb[i + 2, t : t + 8, :] - pb[i, t : t + 8, :]
            )

    start_first(0)

    @pl.loop(0, 4)
    def _(i):
        for zb in range(4):
            s = 8 * zb
            t = Z0 + s
            c = pb[i + 1, t : t + 8, :]
            fore[1, i, s : s + 8, :] = sv[i, s : s + 8, :] - 0.5 * (north(c, -1) - north(c, 1))
            fore[2, i, s : s + 8, :] = sw[i, t : t + 8, :] - 0.5 * (
                pb[i + 1, t + 1 : t + 9, :] - pb[i + 1, t - 1 : t + 7, :]
            )

    start_first(1)
    start_first(2)

    small(totals.at[pl.ds(0, NPEER - 1)], totals.at[pl.ds(0, NPEER - 1)], 2, after).wait()
    a = totals[0:16]
    b = totals[16:32]
    top = jnp.maximum(a, b)
    isle = top + jnp.log(jnp.exp(a - top) + jnp.exp(b - top))
    peak = jnp.max(isle, axis=0)
    whole = peak + jnp.log(jnp.sum(jnp.exp(isle - peak[None]), axis=0))
    a1 = totals[isl]
    b1 = totals[isl + 16]
    top1 = jnp.maximum(a1, b1)
    mine = top1 + jnp.log(jnp.exp(a1 - top1) + jnp.exp(b1 - top1))
    logp[...] = totals[me] - mine
    logi[...] = mine - whole

    for g in range(3):
        start_second(g)
    for g in range(4):
        all_of(g, s1, r1).wait_send()
        all_of(g, s2, r2).wait()


def step(ensemble, observations, obs_precision, island_ancestor, particle_ancestor):
    field = ensemble[0, 0]
    vmem = pl.BlockSpec(memory_space=pltpu.VMEM)
    smem = pl.BlockSpec(memory_space=pltpu.SMEM)
    f32 = jnp.float32
    tall = Z0 + NZ + 8
    dma = pltpu.SemaphoreType.DMA
    out, logp, logi = pl.pallas_call(
        kernel,
        out_shape=(
            jax.ShapeDtypeStruct(field.shape, f32),
            jax.ShapeDtypeStruct((1, 128), f32),
            jax.ShapeDtypeStruct((1, 128), f32),
        ),
        in_specs=[smem, smem, vmem, vmem, pl.BlockSpec(memory_space=pl.ANY)],
        out_specs=(vmem, vmem, vmem),
        scratch_shapes=[pltpu.VMEM((10, tall, LANES), f32) for _ in range(4)]
        + [
            pltpu.VMEM((6, NZ, LANES), f32),
            pltpu.VMEM((4, NZ, LANES), f32),
            pltpu.VMEM((4, tall, LANES), f32),
            pltpu.VMEM((10, tall, LANES), f32),
            pltpu.VMEM((8, tall, LANES), f32),
            pltpu.VMEM((6, tall, LANES), f32),
            pltpu.VMEM((10, tall, LANES), f32),
            pltpu.VMEM((10, tall, LANES), f32),
            pltpu.VMEM((4, 4, NZ, LANES), f32),
        ]
        + [pltpu.VMEM((NPEER, 8, 256), f32) for _ in range(8)]
        + [
            pltpu.VMEM((NPEER, 1, 128), f32),
            pltpu.VMEM((8, 1, 128), f32),
            pltpu.VMEM((NPEER, 1, 128), f32),
            dma((4,)),
            dma((7, 2)),
            dma((7, 2)),
            dma((4,)),
            dma((4,)),
            dma((4,)),
            dma((4,)),
            dma((3,)),
            dma((3,)),
        ],
        compiler_params=pltpu.CompilerParams(
            collective_id=0, has_side_effects=True, vmem_limit_bytes=56 * 1024 * 1024
        ),
    )(island_ancestor, particle_ancestor, observations, obs_precision, field)
    return out[None, None], logp[:, :1], logi[0, :1]


def solution(mesh):
    return jax.shard_map(
        step,
        mesh=mesh,
        in_specs=(
            P("isl", "par", None, "sp", None, None),
            P("sp", None),
            P("sp", None),
            P(),
            P("isl", "par"),
        ),
        out_specs=(P("isl", "par", None, "sp", None, None), P("isl", "par"), P("isl")),
        check_vma=False,
    )
```

time: 140 us -> 87.5 us (0.62); the launches traced: 137 us -> 86.8 us
  waiting for transfers between devices: 48.2 us -> 0 us
  Pallas kernels: 59.6 us -> 81.5 us
  starting transfers between devices: 10.6 us -> 0 us
  local copies, waits for them, and re-layouts: 9.39 us -> 2.32 us
  other arithmetic: 5.99 us -> 0 us
    ppermute x22 -> x0, waiting for transfers between devices: 48.2 us -> none  [the longest x11 41.5 us: extended_2(): lax.ppermute(head, axis, [((i + 1) % count, i) for i in range(count)])]
    pallas_call x1, Pallas kernels: 59.6 us -> 81.5 us  [step(): pl.pallas_call(kernel, out_shape=(jax.ShapeDtypeStruct(field.shape, f32),...]
    ppermute x22 -> x0, starting transfers between devices: 10.6 us -> none  [the longest x11 5.41 us: extended_2(): lax.ppermute(tail, axis, [(i, (i + 1) % count) for i in range(count)])]
    slice x44 -> x0, local copies, waits for them, and re-layouts: 4.94 us -> none  [the longest x16 1.7 us: neighbours(): jnp.roll(middle, -1, -1)]
    add x13 -> x0, other arithmetic: 3.69 us -> none  [the longest x8 1.84 us: sweep(): middle + relaxation * (neighbours(padded) - 6.0 * middle - divergence) / 6.0]
    broadcast_in_dim x2 -> x0, local copies, waits for them, and re-layouts: 1.67 us -> none  [the longest x1 1.16 us: shards(): part = jnp.broadcast_to(partial_value[:, None], (1, 128))]
  transfers between devices with their start and end apart: 22 -> 0, of which waited for: 20 -> 0; matrix products, arithmetic and copies ran while one was open for 2% -> 0% of each run, Pallas kernels for 0% -> 0%
where the time goes in v2:
time: 87.5 us; the launch traced here: 86.8 us
  Pallas kernels  81.5 us (93%)
  between operations  3.01 us (3%)
  local copies, waits for them, and re-layouts  2.32 us (3%)
    pallas_call x1, Pallas kernels, step(): pl.pallas_call(kernel, out_shape=(jax.ShapeDtypeStruct(field.shape, f32),...  81.5 us
    unnamed x5, local copies, waits for them, and re-layouts  2.32 us

profile of v2, /device:TPU:25, one launch (start us, length us, event | category | flops | bytes accessed | tf_op | source)
XLA Modules:
  0.0 86.8 jit_solution(15349618788787263026)
XLA Ops:
  1.3 81.5 %shard_map.76 = (f32[4,4,32,512]{3,2,1,0:T(8,128)}, f32[1,128]{1,0:T(1,128)}, f32[1,128]{1,0:T(1,128)}) custom-call(s32[16]{0:T(128)} %anc.1, s32[1,1]{1,0:T(1,128)S(6)} %copy.11.pick, f32[4,512]{1,0:T(4,128)} %obs.1, f32[4,512]{1,0:T(4,128)} %prec.1, f32[4,4,32,512]{3,2,1,0:T(8,128)} %bitcast.5), custom_call_target="tpu_custom_call" | custom-call | tf_op jit(solution)/shard_map/pallas_call | solution.py:356
  82.7 0.0 copy-start.1
  82.8 2.3 %copy.12 = f32[1,1,4,4,32,512]{5,4,3,2,1,0:T(8,128)} copy(f32[1,1,4,4,32,512]{5,4,3,2,1,0:T(8,128)} %bitcast.6) | data formatting | bytes 2097152
  85.0 0.0 copy-done.1
  85.0 0.0 copy-start
  85.6 0.0 copy-done
Async XLA Ops:
  82.7 2.3 %copy-start.1 = (f32[1,128]{1,0:T(1,128)S(1)}, f32[1,128]{1,0:T(1,128)}, u32[]{:S(2)}) copy-start(f32[1,128]{1,0:T(1,128)} %get-tuple-element.7) | copy-start | bytes 1540
  85.0 0.6 copy-start

commit v3 on v2

v3 whole, which is shorter than its diff:
```python
import jax
import jax.numpy as jnp
from jax import lax
from jax.experimental import pallas as pl
from jax.experimental.pallas import tpu as pltpu
from jax.sharding import PartitionSpec as P

MESH = pl.DeviceIdType.MESH
NPEER = 32
GROUPS = ((3, 1), (1, 2), (0, 1))
STEP = 0.2
VISC = 0.05
STRAT = 1.0
RELAX = 0.8
Z0 = 8
NZ = 32
LANES = 512


def north(q, k):
    return pltpu.roll(q, k % LANES, 1)


def pad_rows(ref, rows):
    zero = jnp.zeros((8, LANES), jnp.float32)

    @pl.loop(0, rows)
    def _(r):
        ref[r, 0:Z0, :] = zero
        ref[r, Z0 + NZ : Z0 + NZ + 8, :] = zero


def chunk_of(ref, first, count, flat):
    row = flat // 8
    level = pl.multiple_of((flat // 2) % 4 * 8, 8)
    lane = pl.multiple_of(flat % 2 * 256, 256)
    return ref.at[pl.ds(first, count), row, pl.ds(level, 8), pl.ds(lane, 256)]


def kernel(
    anc, pick, obs, prec, ens, out, logp, logi,
    xu, xv, xw, xb, su, sv, sw, dv, a1, a2, a3, a4, a8, fore,
    h0, h1, h2, g0, g1, g2, picks, parts, totals,
    lsem, hs, hr, ws, wr, s1, r1, s2, r2, ssem, rsem, met,
):
    held = (h0, h1, h2)
    sent = (g0, g1, g2)
    isl = lax.axis_index("isl")
    par = lax.axis_index("par")
    sp = lax.axis_index("sp")
    me = par * 16 + isl
    z = par * 4 + lax.div(isl, 4)
    x = lax.rem(isl, 4)
    after = {"sp": lax.rem(sp + 1, 8)}
    before = {"sp": lax.rem(sp + 7, 8)}
    fields = (xu, xv, xw, xb)

    zs = []
    for dz in range(8):
        zt = lax.rem(z + dz, 8)
        zs.append((zt, lax.rem(zt, 4) * 4, lax.div(zt, 4)))
    xs = [lax.rem(x + dx, 4) for dx in range(4)]

    def away(dz, dx):
        zt, zlo4, hi = zs[dz % 8]
        return {"isl": zlo4 + xs[dx % 4], "par": hi}

    peers = []
    for dz in range(8):
        for dx in range(4):
            if dz or dx:
                peers.append((zs[dz][0] * 4 + xs[dx], away(dz, dx)))
    mates = [{"sp": lax.rem(sp + k, 8)} for k in range(1, 8)]

    def tell(sem, where):
        pl.semaphore_signal(sem, inc=1, device_id=where, device_id_type=MESH)

    barrier = pltpu.get_barrier_semaphore()
    close = (after, before, away(0, 1), away(0, 3), away(1, 0), away(7, 0))
    for where in close:
        tell(barrier, where)

    loads = [
        pltpu.make_async_copy(ens.at[f], fields[f].at[3:7, Z0 : Z0 + NZ, :], lsem.at[f]) for f in range(4)
    ]
    for f in (3, 1, 2, 0):
        loads[f].start()

    def remote(src, dst, ss, rs, where):
        return pltpu.make_async_remote_copy(
            src_ref=src, dst_ref=dst, send_sem=ss, recv_sem=rs, device_id=where, device_id_type=MESH
        )

    def small(src, dst, sem, where):
        return remote(src, dst, ssem.at[sem], rsem.at[sem], where)

    pl.semaphore_wait(barrier, len(close))

    edges = {}
    for f in (3, 1, 2, 0):
        w = 3 if f == 0 else 2
        edges[f] = (
            remote(ens.at[f, 4 - w : 4], fields[f].at[3 - w : 3, Z0 : Z0 + NZ, :], hs.at[f, 0], hr.at[f, 0], after),
            remote(ens.at[f, 0:w], fields[f].at[7 : 7 + w, Z0 : Z0 + NZ, :], hs.at[f, 1], hr.at[f, 1], before),
        )
        for edge in edges[f]:
            edge.start()

    pad_rows(xb, 10)
    pad_rows(xv, 10)
    pad_rows(xw, 10)
    pad_rows(xu, 10)

    for step_, pairs in enumerate(
        (
            (away(1, 0), away(7, 0)),
            (away(2, 0), away(6, 0)),
            (away(0, 1), away(0, 3)),
            (away(0, 1), away(0, 3)),
        )
    ):
        for where in pairs:
            tell(met.at[step_], where)
        if step_ < 2:
            for where in ((after, before), (mates[1], mates[5]))[step_]:
                tell(met.at[4 + step_], where)
        pl.semaphore_wait(met.at[step_], 2)
        if step_ < 2:
            pl.semaphore_wait(met.at[4 + step_], 2)

    picks[me] = jnp.full((1, 128), pick[0, 0], jnp.int32).astype(jnp.float32)
    for _, where in peers:
        small(picks.at[me], picks.at[me], 0, where).start()

    pad_rows(sw, 4)
    for ref in (dv, a1, a2, a3, a4, a8):
        pad_rows(ref, 12)

    def land(copies):
        for copy in copies:
            copy.wait_recv()

    def tendency(q, r, zb, u, v, w):
        s = Z0 + 8 * zb
        c = q[r, s : s + 8, :]
        xp = q[r + 1, s : s + 8, :]
        xm = q[r - 1, s : s + 8, :]
        xpp = q[r + 2, s : s + 8, :]
        xmm = q[r - 2, s : s + 8, :]
        zp = q[r, s + 1 : s + 9, :]
        zm = q[r, s - 1 : s + 7, :]
        zpp = q[r, s + 2 : s + 10, :]
        zmm = q[r, s - 2 : s + 6, :]
        yp = north(c, -1)
        ym = north(c, 1)
        ypp = north(c, -2)
        ymm = north(c, 2)
        lap = (xp + xm) + (yp + ym) + (zp + zm) - 6.0 * c
        adv = (
            u * (8.0 * (xp - xm) - (xpp - xmm))
            + v * (8.0 * (yp - ym) - (ypp - ymm))
            + w * (8.0 * (zp - zm) - (zpp - zmm))
        )
        return c, (STEP * VISC) * lap - adv

    def winds(r, zb):
        s = Z0 + 8 * zb
        return tuple(q[r, s : s + 8, :] * (STEP / 12.0) for q in (xu, xv, xw))

    def first_copy(g, flat, where):
        f, n = GROUPS[g]
        return remote(chunk_of(fore, f, n, flat), held[g].at[me], s1.at[g], r1.at[g], where)

    def second_copy(g, flat, where):
        f, n = GROUPS[g]
        return remote(sent[g].at[flat], chunk_of(out, f, n, me), s2.at[g], r2.at[g], where)

    def all_of(g, s, r):
        return remote(
            sent[g].at[pl.ds(0, NPEER - 1)], held[g].at[pl.ds(0, NPEER - 1)], s.at[g], r.at[g], after
        )

    def start_first(g):
        f, n = GROUPS[g]
        for flat, where in peers:
            first_copy(g, flat, where).start()
        held[g][me] = chunk_of(fore, f, n, me)[...]

    def start_second(g):
        f, n = GROUPS[g]
        all_of(g, s1, r1).wait_recv()

        @pl.loop(0, NPEER)
        def _(d):
            src = anc[lax.rem(d, 16)]
            choose = jnp.broadcast_to(picks[d][None], (n, 8, 128)) < 0.5
            for h in range(2):
                lanes = slice(h * 128, (h + 1) * 128)
                lo = held[g][src, :, :, lanes]
                hi = held[g][src + 16, :, :, lanes]
                sent[g][d, :, :, lanes] = jnp.where(choose, lo, hi)

        for flat, where in peers:
            second_copy(g, flat, where).start()
        chunk_of(out, f, n, me)[...] = sent[g][me]

    for load in loads[:3]:
        load.wait()
    loads[3].wait()
    land(edges[3])

    @pl.loop(0, 4)
    def _(i):
        r = i + 3
        for zb in range(4):
            s = 8 * zb
            u, v, w = winds(r, zb)
            c, g = tendency(xb, r, zb, u, v, w)
            flow = xw[r, Z0 + s : Z0 + s + 8, :]
            fore[3, i, s : s + 8, :] = c + g - (STEP * STRAT) * flow

    start_first(0)

    land(edges[1])

    @pl.loop(0, 4)
    def _(i):
        r = i + 3
        for zb in range(4):
            s = 8 * zb
            u, v, w = winds(r, zb)
            c, g = tendency(xv, r, zb, u, v, w)
            star = c + g
            sv[i, s : s + 8, :] = star
            dv[i + 4, Z0 + s : Z0 + s + 8, :] = 0.5 * (north(star, -1) - north(star, 1))

    land(edges[2])

    @pl.loop(0, 4)
    def _(i):
        r = i + 3
        for zb in range(4):
            s = 8 * zb
            u, v, w = winds(r, zb)
            c, g = tendency(xw, r, zb, u, v, w)
            sw[i, Z0 + s : Z0 + s + 8, :] = c + g + STEP * xb[r, Z0 + s : Z0 + s + 8, :]

    land(edges[0])

    @pl.loop(0, 6)
    def _(i):
        r = i + 2
        for zb in range(4):
            s = 8 * zb
            u, v, w = winds(r, zb)
            c, g = tendency(xu, r, zb, u, v, w)
            su[i, s : s + 8, :] = c + g

    @pl.loop(0, 4)
    def _(i):
        for zb in range(4):
            s = 8 * zb
            t = Z0 + s
            dx = 0.5 * (su[i + 2, s : s + 8, :] - su[i, s : s + 8, :])
            dz = 0.5 * (sw[i, t + 1 : t + 9, :] - sw[i, t - 1 : t + 7, :])
            dv[i + 4, t : t + 8, :] = dx + dv[i + 4, t : t + 8, :] + dz

    def ship(buf, e, away_rows):
        copies = {}
        for j in away_rows:
            copies[j] = (
                remote(
                    buf.at[8 - j, Z0 : Z0 + NZ, :], buf.at[4 - j, Z0 : Z0 + NZ, :], ws.at[e, j, 0], wr.at[e, j, 0], after
                ),
                remote(
                    buf.at[3 + j, Z0 : Z0 + NZ, :], buf.at[7 + j, Z0 : Z0 + NZ, :], ws.at[e, j, 1], wr.at[e, j, 1], before
                ),
            )
            for copy in copies[j]:
                copy.start()
        return copies

    def sweep_row(src, dst, row, first):
        for zb in range(4):
            t = Z0 + 8 * zb
            c = src[row, t : t + 8, :]
            near = (
                (src[row + 1, t : t + 8, :] + src[row - 1, t : t + 8, :])
                + (north(c, 1) + north(c, -1))
                + (src[row, t + 1 : t + 9, :] + src[row, t - 1 : t + 7, :])
            )
            if first:
                k = -RELAX / 6.0
                val = (k * (1.0 - RELAX) - RELAX / 6.0) * c + (k * RELAX / 6.0) * near
            else:
                val = (1.0 - RELAX) * c + (RELAX / 6.0) * (near - dv[row, t : t + 8, :])
            dst[row, t : t + 8, :] = val

    def inner(levels, k, first):
        @pl.loop(0, 2)
        def _(side):
            sweep_row(levels[k - 1], levels[k], 5 + side, first and k == 1)

    def wave(levels, j, first):
        for k in range(1, j + 1):
            d = j - k

            @pl.loop(0, 2)
            def _(side):
                sweep_row(levels[k - 1], levels[k], 4 - d + side * (3 + 2 * d), first and k == 1)

        if j < 4:
            inner(levels, j + 1, first)

    stage = (dv, a1, a2, a3, a4)
    moving = ship(dv, 0, (1, 2, 3, 4))
    inner(stage, 1, True)

    acc = jnp.zeros((1, LANES), jnp.float32)
    for i in range(4):
        gap = fore[3, i, NZ - 1 : NZ, :] - obs[i : i + 1, :]
        ramp = 1.0 + (sp * 4 + i).astype(jnp.float32) * (2.0 / 31.0)
        acc = acc + gap * gap * (prec[i : i + 1, :] * ramp)
    parts[sp] = jnp.broadcast_to(jnp.sum(acc, axis=1, keepdims=True), (1, 128))
    for where in mates:
        small(parts.at[sp], parts.at[sp], 1, where).start()

    for j in (1, 2, 3):
        land(moving[j])
        wave(stage, j, True)
    later = ship(a4, 1, (2, 3))
    land(moving[4])
    wave(stage, 4, True)
    later.update(ship(a4, 1, (1, 4)))

    stage2 = (a4, a1, a2, a3, a8)
    inner(stage2, 1, False)

    small(picks.at[pl.ds(0, NPEER - 1)], picks.at[pl.ds(0, NPEER - 1)], 0, after).wait()
    start_second(0)

    for j in (2, 3, 1):
        land(later[j])
    for j in (1, 2, 3):
        wave(stage2, j, False)
    land(later[4])
    wave(stage2, 4, False)
    last = ship(a8, 2, (1,))

    @pl.loop(0, 4)
    def _(i):
        for zb in range(4):
            s = 8 * zb
            t = Z0 + s
            c = a8[i + 4, t : t + 8, :]
            fore[1, i, s : s + 8, :] = sv[i, s : s + 8, :] - 0.5 * (north(c, -1) - north(c, 1))
            fore[2, i, s : s + 8, :] = sw[i, t : t + 8, :] - 0.5 * (
                a8[i + 4, t + 1 : t + 9, :] - a8[i + 4, t - 1 : t + 7, :]
            )

    start_first(1)

    land(last[1])

    @pl.loop(0, 4)
    def _(i):
        for zb in range(4):
            s = 8 * zb
            t = Z0 + s
            fore[0, i, s : s + 8, :] = su[i + 1, s : s + 8, :] - 0.5 * (
                a8[i + 5, t : t + 8, :] - a8[i + 3, t : t + 8, :]
            )

    start_first(2)

    small(parts.at[pl.ds(0, 7)], parts.at[pl.ds(0, 7)], 1, after).wait()
    mis = parts[0]
    for k in range(1, 8):
        mis = mis + parts[k]
    totals[me] = -0.5 * mis
    for _, where in peers:
        small(totals.at[me], totals.at[me], 2, where).start()

    start_second(1)

    small(totals.at[pl.ds(0, NPEER - 1)], totals.at[pl.ds(0, NPEER - 1)], 2, after).wait()
    a = totals[0:16]
    b = totals[16:32]
    top = jnp.maximum(a, b)
    isle = top + jnp.log(jnp.exp(a - top) + jnp.exp(b - top))
    peak = jnp.max(isle, axis=0)
    whole = peak + jnp.log(jnp.sum(jnp.exp(isle - peak[None]), axis=0))
    own = totals[isl]
    other = totals[isl + 16]
    top1 = jnp.maximum(own, other)
    mine = top1 + jnp.log(jnp.exp(own - top1) + jnp.exp(other - top1))
    logp[...] = totals[me] - mine
    logi[...] = mine - whole

    start_second(2)

    for f in range(4):
        for edge in edges[f]:
            edge.wait_send()
    for group in (moving, later, last):
        for copies in group.values():
            for copy in copies:
                copy.wait_send()
    for g in range(3):
        all_of(g, s1, r1).wait_send()
        all_of(g, s2, r2).wait()


def step(ensemble, observations, obs_precision, island_ancestor, particle_ancestor):
    field = ensemble[0, 0]
    vmem = pl.BlockSpec(memory_space=pltpu.VMEM)
    smem = pl.BlockSpec(memory_space=pltpu.SMEM)
    f32 = jnp.float32
    tall = Z0 + NZ + 8
    dma = pltpu.SemaphoreType.DMA
    out, logp, logi = pl.pallas_call(
        kernel,
        out_shape=(
            jax.ShapeDtypeStruct(field.shape, f32),
            jax.ShapeDtypeStruct((1, 128), f32),
            jax.ShapeDtypeStruct((1, 128), f32),
        ),
        in_specs=[smem, smem, vmem, vmem, pl.BlockSpec(memory_space=pl.ANY)],
        out_specs=(vmem, vmem, vmem),
        scratch_shapes=[pltpu.VMEM((10, tall, LANES), f32) for _ in range(4)]
        + [
            pltpu.VMEM((6, NZ, LANES), f32),
            pltpu.VMEM((4, NZ, LANES), f32),
            pltpu.VMEM((4, tall, LANES), f32),
        ]
        + [pltpu.VMEM((12, tall, LANES), f32) for _ in range(6)]
        + [pltpu.VMEM((4, 4, NZ, LANES), f32)]
        + [pltpu.VMEM((NPEER, n, 8, 256), f32) for _, n in GROUPS + GROUPS]
        + [
            pltpu.VMEM((NPEER, 1, 128), f32),
            pltpu.VMEM((8, 1, 128), f32),
            pltpu.VMEM((NPEER, 1, 128), f32),
            dma((4,)),
            dma((4, 2)),
            dma((4, 2)),
            dma((3, 5, 2)),
            dma((3, 5, 2)),
            dma((3,)),
            dma((3,)),
            dma((3,)),
            dma((3,)),
            dma((3,)),
            dma((3,)),
            pltpu.SemaphoreType.REGULAR((6,)),
        ],
        compiler_params=pltpu.CompilerParams(
            collective_id=0, has_side_effects=True, vmem_limit_bytes=56 * 1024 * 1024
        ),
    )(island_ancestor, particle_ancestor, observations, obs_precision, field)
    return out[None, None], logp[:, :1], logi[0, :1]


def solution(mesh):
    return jax.shard_map(
        step,
        mesh=mesh,
        in_specs=(
            P("isl", "par", None, "sp", None, None),
            P("sp", None),
            P("sp", None),
            P(),
            P("isl", "par"),
        ),
        out_specs=(P("isl", "par", None, "sp", None, None), P("isl", "par"), P("isl")),
        check_vma=False,
    )
```

time: 87.5 us -> 79 us (0.903)
  Pallas kernels: 81.5 us -> 73.5 us
    pallas_call x1, Pallas kernels: 81.5 us -> 73.5 us  [step(): pl.pallas_call(kernel, out_shape=(jax.ShapeDtypeStruct(field.shape, f32),...]
where the time goes in v3:
time: 79 us; the launch traced here: 78.9 us
  Pallas kernels  73.5 us (93%)
  between operations  3.01 us (4%)
  local copies, waits for them, and re-layouts  2.32 us (3%)
    pallas_call x1, Pallas kernels, step(): pl.pallas_call(kernel, out_shape=(jax.ShapeDtypeStruct(field.shape, f32),...  73.5 us
    unnamed x5, local copies, waits for them, and re-layouts  2.32 us

profile of v3, /device:TPU:25, one launch (start us, length us, event | category | flops | bytes accessed | tf_op | source)
XLA Modules:
  0.0 78.9 jit_solution(5082060126480334089)
XLA Ops:
  1.3 73.5 %shard_map.76 = (f32[4,4,32,512]{3,2,1,0:T(8,128)}, f32[1,128]{1,0:T(1,128)}, f32[1,128]{1,0:T(1,128)}) custom-call(s32[16]{0:T(128)} %anc.1, s32[1,1]{1,0:T(1,128)S(6)} %copy.11.pick, f32[4,512]{1,0:T(4,128)} %obs.1, f32[4,512]{1,0:T(4,128)} %prec.1, f32[4,4,32,512]{3,2,1,0:T(8,128)} %bitcast.5), custom_call_target="tpu_custom_call" | custom-call | tf_op jit(solution)/shard_map/pallas_call | solution.py:421
  74.8 0.0 copy-start.1
  74.8 2.3 %copy.12 = f32[1,1,4,4,32,512]{5,4,3,2,1,0:T(8,128)} copy(f32[1,1,4,4,32,512]{5,4,3,2,1,0:T(8,128)} %bitcast.6) | data formatting | bytes 2097152
  77.1 0.0 copy-done.1
  77.1 0.0 copy-start
  77.7 0.0 copy-done
Async XLA Ops:
  74.8 2.3 %copy-start.1 = (f32[1,128]{1,0:T(1,128)S(1)}, f32[1,128]{1,0:T(1,128)}, u32[]{:S(2)}) copy-start(f32[1,128]{1,0:T(1,128)} %get-tuple-element.7) | copy-start | bytes 1540
  77.1 0.6 copy-start

commit v4 on v3

--- a/solution.py
+++ b/solution.py
@@ -13,6 +13,10 @@
 STRAT = 1.0
 RELAX = 0.8
 Z0 = 8
+FAR_FIRST = sorted(
+    [(dz, dx) for dz in range(8) for dx in range(4) if dz or dx],
+    key=lambda k: -(min(k[0], 8 - k[0]) + min(k[1], 4 - k[1])),
+)
 NZ = 32
 LANES = 512
 
@@ -66,10 +70,8 @@
         return {"isl": zlo4 + xs[dx % 4], "par": hi}
 
     peers = []
-    for dz in range(8):
-        for dx in range(4):
-            if dz or dx:
-                peers.append((zs[dz][0] * 4 + xs[dx], away(dz, dx)))
+    for dz, dx in FAR_FIRST:
+        peers.append((zs[dz][0] * 4 + xs[dx], away(dz, dx)))
     mates = [{"sp": lax.rem(sp + k, 8)} for k in range(1, 8)]
 
     def tell(sem, where):
@@ -106,35 +108,32 @@
         for edge in edges[f]:
             edge.start()
 
+    rounds = (
+        (away(1, 0), away(7, 0), away(0, 1), away(0, 3), after, before),
+        (away(2, 0), away(6, 0), mates[1], mates[5]),
+        (away(0, 1), away(0, 3), away(0, 2)),
+    )
+
+    def call(k):
+        for where in rounds[k]:
+            tell(met.at[k], where)
+
+    def hear(k):
+        pl.semaphore_wait(met.at[k], len(rounds[k]))
+
+    call(0)
     pad_rows(xb, 10)
     pad_rows(xv, 10)
     pad_rows(xw, 10)
     pad_rows(xu, 10)
-
-    for step_, pairs in enumerate(
-        (
-            (away(1, 0), away(7, 0)),
-            (away(2, 0), away(6, 0)),
-            (away(0, 1), away(0, 3)),
-            (away(0, 1), away(0, 3)),
-        )
-    ):
-        for where in pairs:
-            tell(met.at[step_], where)
-        if step_ < 2:
-            for where in ((after, before), (mates[1], mates[5]))[step_]:
-                tell(met.at[4 + step_], where)
-        pl.semaphore_wait(met.at[step_], 2)
-        if step_ < 2:
-            pl.semaphore_wait(met.at[4 + step_], 2)
-
-    picks[me] = jnp.full((1, 128), pick[0, 0], jnp.int32).astype(jnp.float32)
-    for _, where in peers:
-        small(picks.at[me], picks.at[me], 0, where).start()
-
+    hear(0)
+    call(1)
     pad_rows(sw, 4)
     for ref in (dv, a1, a2, a3, a4, a8):
         pad_rows(ref, 12)
+    picks[me] = jnp.full((1, 128), pick[0, 0], jnp.int32).astype(jnp.float32)
+    hear(1)
+    call(2)
 
     def land(copies):
         for copy in copies:
@@ -163,13 +162,17 @@
         )
         return c, (STEP * VISC) * lap - adv
 
+    def put(f, i, zb, value):
+        fore[f, i * 8 + zb * 2] = value[:, 0:256]
+        fore[f, i * 8 + zb * 2 + 1] = value[:, 256:512]
+
     def winds(r, zb):
         s = Z0 + 8 * zb
         return tuple(q[r, s : s + 8, :] * (STEP / 12.0) for q in (xu, xv, xw))
 
     def first_copy(g, flat, where):
         f, n = GROUPS[g]
-        return remote(chunk_of(fore, f, n, flat), held[g].at[me], s1.at[g], r1.at[g], where)
+        return remote(fore.at[pl.ds(f, n), flat], held[g].at[me], s1.at[g], r1.at[g], where)
 
     def second_copy(g, flat, where):
         f, n = GROUPS[g]
@@ -184,7 +187,7 @@
         f, n = GROUPS[g]
         for flat, where in peers:
             first_copy(g, flat, where).start()
-        held[g][me] = chunk_of(fore, f, n, me)[...]
+        held[g][me] = fore[pl.ds(f, n), me]
 
     def start_second(g):
         f, n = GROUPS[g]
@@ -217,9 +220,12 @@
             u, v, w = winds(r, zb)
             c, g = tendency(xb, r, zb, u, v, w)
             flow = xw[r, Z0 + s : Z0 + s + 8, :]
-            fore[3, i, s : s + 8, :] = c + g - (STEP * STRAT) * flow
-
+            put(3, i, zb, c + g - (STEP * STRAT) * flow)
+
+    hear(2)
     start_first(0)
+    for _, where in peers:
+        small(picks.at[me], picks.at[me], 0, where).start()
 
     land(edges[1])
 
@@ -316,11 +322,13 @@
     moving = ship(dv, 0, (1, 2, 3, 4))
     inner(stage, 1, True)
 
-    acc = jnp.zeros((1, LANES), jnp.float32)
+    acc = jnp.zeros((1, 256), jnp.float32)
     for i in range(4):
-        gap = fore[3, i, NZ - 1 : NZ, :] - obs[i : i + 1, :]
         ramp = 1.0 + (sp * 4 + i).astype(jnp.float32) * (2.0 / 31.0)
-        acc = acc + gap * gap * (prec[i : i + 1, :] * ramp)
+        for h in range(2):
+            lanes = slice(h * 256, (h + 1) * 256)
+            gap = fore[3, i * 8 + 6 + h, 7:8, :] - obs[i : i + 1, lanes]
+            acc = acc + gap * gap * (prec[i : i + 1, lanes] * ramp)
     parts[sp] = jnp.broadcast_to(jnp.sum(acc, axis=1, keepdims=True), (1, 128))
     for where in mates:
         small(parts.at[sp], parts.at[sp], 1, where).start()
@@ -353,10 +361,9 @@
             s = 8 * zb
             t = Z0 + s
             c = a8[i + 4, t : t + 8, :]
-            fore[1, i, s : s + 8, :] = sv[i, s : s + 8, :] - 0.5 * (north(c, -1) - north(c, 1))
-            fore[2, i, s : s + 8, :] = sw[i, t : t + 8, :] - 0.5 * (
-                a8[i + 4, t + 1 : t + 9, :] - a8[i + 4, t - 1 : t + 7, :]
-            )
+            put(1, i, zb, sv[i, s : s + 8, :] - 0.5 * (north(c, -1) - north(c, 1)))
+            grad = a8[i + 4, t + 1 : t + 9, :] - a8[i + 4, t - 1 : t + 7, :]
+            put(2, i, zb, sw[i, t : t + 8, :] - 0.5 * grad)
 
     start_first(1)
 
@@ -367,9 +374,8 @@
         for zb in range(4):
             s = 8 * zb
             t = Z0 + s
-            fore[0, i, s : s + 8, :] = su[i + 1, s : s + 8, :] - 0.5 * (
-                a8[i + 5, t : t + 8, :] - a8[i + 3, t : t + 8, :]
-            )
+            grad = a8[i + 5, t : t + 8, :] - a8[i + 3, t : t + 8, :]
+            put(0, i, zb, su[i + 1, s : s + 8, :] - 0.5 * grad)
 
     start_first(2)
 
@@ -421,7 +427,7 @@
     out, logp, logi = pl.pallas_call(
         kernel,
         out_shape=(
-            jax.ShapeDtypeStruct(field.shape, f32),
+            pltpu.VMEM(field.shape, f32),
             jax.ShapeDtypeStruct((1, 128), f32),
             jax.ShapeDtypeStruct((1, 128), f32),
         ),
@@ -434,7 +440,7 @@
             pltpu.VMEM((4, tall, LANES), f32),
         ]
         + [pltpu.VMEM((12, tall, LANES), f32) for _ in range(6)]
-        + [pltpu.VMEM((4, 4, NZ, LANES), f32)]
+        + [pltpu.VMEM((4, NPEER, 8, 256), f32)]
         + [pltpu.VMEM((NPEER, n, 8, 256), f32) for _, n in GROUPS + GROUPS]
         + [
             pltpu.VMEM((NPEER, 1, 128), f32),
@@ -451,7 +457,7 @@
             dma((3,)),
             dma((3,)),
             dma((3,)),
-            pltpu.SemaphoreType.REGULAR((6,)),
+            pltpu.SemaphoreType.REGULAR((3,)),
         ],
         compiler_params=pltpu.CompilerParams(
             collective_id=0, has_side_effects=True, vmem_limit_bytes=56 * 1024 * 1024

time: 79 us -> 73.3 us (0.928)
  Pallas kernels: 73.5 us -> 68.9 us
  local copies, waits for them, and re-layouts: 2.32 us -> 1.07 us
    pallas_call x1, Pallas kernels: 73.5 us -> 68.9 us  [step(): pl.pallas_call(kernel, out_shape=(pltpu.VMEM(field.shape, f32), jax.Shape...]
    unnamed x5, local copies, waits for them, and re-layouts: 2.32 us -> 1.07 us
where the time goes in v4:
time: 73.3 us; the launch traced here: 72.9 us
  Pallas kernels  68.9 us (94%)
  between operations  3.01 us (4%)
  local copies, waits for them, and re-layouts  1.07 us (1%)
    pallas_call x1, Pallas kernels, step(): pl.pallas_call(kernel, out_shape=(pltpu.VMEM(field.shape, f32), jax.Shape...  68.9 us

profile of v4, /device:TPU:25, one launch (start us, length us, event | category | flops | bytes accessed | tf_op | source)
XLA Modules:
  0.0 72.9 jit_solution(8438641281950645598)
XLA Ops:
  1.3 68.9 %shard_map.76 = (f32[4,4,32,512]{3,2,1,0:T(8,128)S(1)}, f32[1,128]{1,0:T(1,128)}, f32[1,128]{1,0:T(1,128)}) custom-call(s32[16]{0:T(128)} %anc.1, s32[1,1]{1,0:T(1,128)S(6)} %copy.12.pick, f32[4,512]{1,0:T(4,128)} %obs.1, f32[4,512]{1,0:T(4,128)} %prec.1, f32[4,4,32,512]{3,2,1,0:T(8,128)} %bitcast.6), custom_call_target="tpu_custom_call" | custom-call | tf_op jit(solution)/shard_map/pallas_call | solution.py:427
  70.1 0.0 copy-start.1
  70.2 1.0 %copy.11 = f32[1,1,4,4,32,512]{5,4,3,2,1,0:T(8,128)} copy(f32[1,1,4,4,32,512]{5,4,3,2,1,0:T(8,128)S(1)} %bitcast.5) | data formatting | bytes 2097152
  71.1 0.0 copy-done.1
  71.1 0.0 copy-start
  71.7 0.1 copy-done
Async XLA Ops:
  70.1 1.0 %copy-start.1 = (f32[1,128]{1,0:T(1,128)S(1)}, f32[1,128]{1,0:T(1,128)}, u32[]{:S(2)}) copy-start(f32[1,128]{1,0:T(1,128)} %get-tuple-element.7) | copy-start | bytes 1540
  71.1 0.6 copy-start

commit v5 on v4

v5 whole, which is shorter than its diff:
```python
import jax
import jax.numpy as jnp
from jax import lax
from jax.experimental import pallas as pl
from jax.experimental.pallas import tpu as pltpu
from jax.sharding import PartitionSpec as P

MESH = pl.DeviceIdType.MESH
NPEER = 32
GROUPS = ((3, 1), (1, 2), (0, 1))
STEP = 0.2
VISC = 0.05
STRAT = 1.0
RELAX = 0.8
Z0 = 8
FAR_FIRST = sorted(
    [(dz, dx) for dz in range(8) for dx in range(4) if dz or dx],
    key=lambda k: -(min(k[0], 8 - k[0]) + min(k[1], 4 - k[1])),
)
NZ = 32
LANES = 512


def north(q, k):
    return pltpu.roll(q, k % LANES, 1)


def pad_rows(ref, rows):
    zero = jnp.zeros((4, 8, 128), jnp.float32)

    @pl.loop(0, rows)
    def _(r):
        ref[r, :, 0:Z0, :] = zero
        ref[r, :, Z0 + NZ : Z0 + NZ + 8, :] = zero


def level(q, r, k, off=0):
    rows = pl.ds(Z0 + k + off, 8, stride=4)
    return jnp.concatenate([q[r, lane, rows, :] for lane in range(4)], axis=1)


def upper(tile):
    place = lax.broadcasted_iota(jnp.int32, tile.shape, 0)
    return jnp.where(place == 7, 0.0, pltpu.roll(tile, 7, 0))


def lower(tile):
    place = lax.broadcasted_iota(jnp.int32, tile.shape, 0)
    return jnp.where(place == 0, 0.0, pltpu.roll(tile, 1, 0))


def chunk_of(ref, first, count, flat):
    row = flat // 8
    lane = pl.multiple_of((flat // 2) % 4 * 128, 128)
    start = pl.multiple_of(flat % 2 * 16, 16)
    return ref.at[pl.ds(first, count), row, pl.ds(start, 16), pl.ds(lane, 128)]


def kernel(
    anc_far, pick, obs_far, prec_far, ens, out, logp, logi,
    xu, xv, xw, xb, su, sv, sw, dv, a1, a2, a3, a4, a8, fore,
    h0, h1, h2, g0, g1, g2, picks, parts, totals,
    anc, obs, prec, lsem, hs, hr, ws, wr, s1, r1, s2, r2, ssem, rsem, met,
):
    held = (h0, h1, h2)
    sent = (g0, g1, g2)
    isl = lax.axis_index("isl")
    par = lax.axis_index("par")
    sp = lax.axis_index("sp")
    me = par * 16 + isl
    z = par * 4 + lax.div(isl, 4)
    x = lax.rem(isl, 4)
    after = {"sp": lax.rem(sp + 1, 8)}
    before = {"sp": lax.rem(sp + 7, 8)}
    fields = (xu, xv, xw, xb)

    zs = []
    for dz in range(8):
        zt = lax.rem(z + dz, 8)
        zs.append((zt, lax.rem(zt, 4) * 4, lax.div(zt, 4)))
    xs = [lax.rem(x + dx, 4) for dx in range(4)]

    def away(dz, dx):
        zt, zlo4, hi = zs[dz % 8]
        return {"isl": zlo4 + xs[dx % 4], "par": hi}

    peers = []
    for dz, dx in FAR_FIRST:
        peers.append((zs[dz][0] * 4 + xs[dx], away(dz, dx)))
    mates = [{"sp": lax.rem(sp + k, 8)} for k in range(1, 8)]

    def tell(sem, where):
        pl.semaphore_signal(sem, inc=1, device_id=where, device_id_type=MESH)

    barrier = pltpu.get_barrier_semaphore()
    close = (after, before, away(0, 1), away(0, 3), away(1, 0), away(7, 0))
    for where in close:
        tell(barrier, where)

    loads = [
        pltpu.make_async_copy(
            ens.at[f, :, :, pl.ds(lane * 128, 128)], fields[f].at[3:7, lane, Z0 : Z0 + NZ, :], lsem.at[f, lane]
        )
        for f in (3, 1, 2, 0)
        for lane in range(4)
    ]
    loads += [
        pltpu.make_async_copy(obs_far, obs, lsem.at[4, 0]),
        pltpu.make_async_copy(prec_far, prec, lsem.at[4, 1]),
        pltpu.make_async_copy(anc_far, anc, lsem.at[4, 2]),
    ]
    for load in loads:
        load.start()

    def remote(src, dst, ss, rs, where):
        return pltpu.make_async_remote_copy(
            src_ref=src, dst_ref=dst, send_sem=ss, recv_sem=rs, device_id=where, device_id_type=MESH
        )

    def small(src, dst, sem, where):
        return remote(src, dst, ssem.at[sem], rsem.at[sem], where)

    pl.semaphore_wait(barrier, len(close))

    edges = {}
    for f in (3, 1, 2, 0):
        w = 3 if f == 0 else 2
        edges[f] = []
        for lane in range(4):
            cut = pl.ds(lane * 128, 128)
            into = fields[f].at[:, lane, Z0 : Z0 + NZ, :]
            edges[f] += [
                remote(
                    ens.at[f, 4 - w : 4, :, cut], into.at[3 - w : 3], hs.at[f, 0, lane], hr.at[f, 0, lane], after
                ),
                remote(ens.at[f, 0:w, :, cut], into.at[7 : 7 + w], hs.at[f, 1, lane], hr.at[f, 1, lane], before),
            ]
        for edge in edges[f]:
            edge.start()

    rounds = (
        (away(1, 0), away(7, 0), away(0, 1), away(0, 3), after, before),
        (away(2, 0), away(6, 0), mates[1], mates[5]),
        (away(0, 1), away(0, 3), away(0, 2)),
    )

    def call(k):
        for where in rounds[k]:
            tell(met.at[k], where)

    def hear(k):
        pl.semaphore_wait(met.at[k], len(rounds[k]))

    call(0)
    pad_rows(xb, 10)
    pad_rows(xv, 10)
    pad_rows(xw, 10)
    pad_rows(xu, 10)
    hear(0)
    call(1)
    picks[me] = jnp.full((1, 128), pick[0, 0], jnp.int32).astype(jnp.float32)
    hear(1)
    call(2)

    def land(copies):
        for copy in copies:
            copy.wait_recv()

    def tendency(q, r, k, u, v, w):
        c = level(q, r, k, 0)
        xp = level(q, r + 1, k, 0)
        xm = level(q, r - 1, k, 0)
        xpp = level(q, r + 2, k, 0)
        xmm = level(q, r - 2, k, 0)
        zp = level(q, r, k, 1)
        zm = level(q, r, k, -1)
        zpp = level(q, r, k, 2)
        zmm = level(q, r, k, -2)
        yp = north(c, -1)
        ym = north(c, 1)
        ypp = north(c, -2)
        ymm = north(c, 2)
        lap = (xp + xm) + (yp + ym) + (zp + zm) - 6.0 * c
        adv = (
            u * (8.0 * (xp - xm) - (xpp - xmm))
            + v * (8.0 * (yp - ym) - (ypp - ymm))
            + w * (8.0 * (zp - zm) - (zpp - zmm))
        )
        return c, (STEP * VISC) * lap - adv

    def put(f, i, k, value):
        for lane in range(4):
            fore[f, pl.ds((i * 4 + lane) * NZ + k, 8, stride=4), :] = value[:, lane * 128 : (lane + 1) * 128]

    def winds(r, k):
        return tuple(level(q, r, k, 0) * (STEP / 12.0) for q in (xu, xv, xw))

    def first_copy(g, flat, where):
        f, n = GROUPS[g]
        return remote(fore.at[pl.ds(f, n), pl.ds(pl.multiple_of(flat * 16, 16), 16), :], held[g].at[me], s1.at[g], r1.at[g], where)

    def second_copy(g, flat, where):
        f, n = GROUPS[g]
        return remote(sent[g].at[flat], chunk_of(out, f, n, me), s2.at[g], r2.at[g], where)

    def all_of(g, s, r):
        return remote(
            sent[g].at[pl.ds(0, NPEER - 1)], held[g].at[pl.ds(0, NPEER - 1)], s.at[g], r.at[g], after
        )

    def start_first(g):
        f, n = GROUPS[g]
        for flat, where in peers:
            first_copy(g, flat, where).start()
        held[g][me] = fore[pl.ds(f, n), pl.ds(pl.multiple_of(me * 16, 16), 16), :]

    def start_second(g):
        f, n = GROUPS[g]
        all_of(g, s1, r1).wait_recv()

        @pl.loop(0, NPEER)
        def _(d):
            src = anc[lax.rem(d, 16)]
            choose = jnp.broadcast_to(picks[d][None], (n, 16, 128)) < 0.5
            sent[g][d] = jnp.where(choose, held[g][src], held[g][src + 16])

        for flat, where in peers:
            second_copy(g, flat, where).start()
        chunk_of(out, f, n, me)[...] = sent[g][me]

    for load in loads:
        load.wait()
    land(edges[3])

    @pl.loop(0, 4)
    def _(i):
        r = i + 3
        for k in range(4):
            u, v, w = winds(r, k)
            c, g = tendency(xb, r, k, u, v, w)
            put(3, i, k, c + g - (STEP * STRAT) * level(xw, r, k, 0))

    hear(2)
    start_first(0)
    for _, where in peers:
        small(picks.at[me], picks.at[me], 0, where).start()

    land(edges[1])

    @pl.loop(0, 4)
    def _(i):
        r = i + 3
        for k in range(4):
            u, v, w = winds(r, k)
            c, g = tendency(xv, r, k, u, v, w)
            star = c + g
            sv[i, 8 * k : 8 * k + 8, :] = star
            dv[i + 4, 8 * k : 8 * k + 8, :] = 0.5 * (north(star, -1) - north(star, 1))

    land(edges[2])

    @pl.loop(0, 4)
    def _(i):
        r = i + 3
        for k in range(4):
            u, v, w = winds(r, k)
            c, g = tendency(xw, r, k, u, v, w)
            star = c + g + STEP * level(xb, r, k, 0)
            sw[i, 8 * k : 8 * k + 8, :] = star
        tiles = [sw[i, 8 * k : 8 * k + 8, :] for k in range(4)]
        above = (tiles[1], tiles[2], tiles[3], upper(tiles[0]))
        below = (lower(tiles[3]), tiles[0], tiles[1], tiles[2])
        for k in range(4):
            dv[i + 4, 8 * k : 8 * k + 8, :] = dv[i + 4, 8 * k : 8 * k + 8, :] + 0.5 * (above[k] - below[k])

    land(edges[0])

    @pl.loop(0, 6)
    def _(i):
        r = i + 2
        for k in range(4):
            u, v, w = winds(r, k)
            c, g = tendency(xu, r, k, u, v, w)
            su[i, 8 * k : 8 * k + 8, :] = c + g

    @pl.loop(0, 4)
    def _(i):
        for k in range(4):
            s = slice(8 * k, 8 * k + 8)
            dv[i + 4, s, :] = dv[i + 4, s, :] + 0.5 * (su[i + 2, s, :] - su[i, s, :])

    def ship(buf, e, away_rows):
        copies = {}
        for j in away_rows:
            copies[j] = (
                remote(
                    buf.at[8 - j], buf.at[4 - j], ws.at[e, j, 0], wr.at[e, j, 0], after
                ),
                remote(
                    buf.at[3 + j], buf.at[7 + j], ws.at[e, j, 1], wr.at[e, j, 1], before
                ),
            )
            for copy in copies[j]:
                copy.start()
        return copies

    def sweep_row(src, dst, row, first):
        tiles = [src[row, 8 * k : 8 * k + 8, :] for k in range(4)]
        above = (tiles[1], tiles[2], tiles[3], upper(tiles[0]))
        below = (lower(tiles[3]), tiles[0], tiles[1], tiles[2])
        for k in range(4):
            s = slice(8 * k, 8 * k + 8)
            c = tiles[k]
            near = (src[row + 1, s, :] + src[row - 1, s, :]) + (north(c, 1) + north(c, -1)) + (above[k] + below[k])
            if first:
                m = -RELAX / 6.0
                val = (m * (1.0 - RELAX) - RELAX / 6.0) * c + (m * RELAX / 6.0) * near
            else:
                val = (1.0 - RELAX) * c + (RELAX / 6.0) * (near - dv[row, s, :])
            dst[row, s, :] = val

    def inner(levels, k, first):
        for row in (5, 6):
            sweep_row(levels[k - 1], levels[k], row, first and k == 1)

    def wave(levels, j, first):
        for k in range(1, j + 1):
            for row in (4 - j + k, 7 + j - k):
                sweep_row(levels[k - 1], levels[k], row, first and k == 1)

        if j < 4:
            inner(levels, j + 1, first)

    stage = (dv, a1, a2, a3, a4)
    moving = ship(dv, 0, (1, 2, 3, 4))
    inner(stage, 1, True)

    acc = jnp.zeros((1, 128), jnp.float32)
    for i in range(4):
        ramp = 1.0 + (sp * 4 + i).astype(jnp.float32) * (2.0 / 31.0)
        for lane in range(4):
            lanes = slice(lane * 128, (lane + 1) * 128)
            top_row = (i * 4 + lane) * NZ + NZ - 1
            gap = fore[3, top_row : top_row + 1, :] - obs[i : i + 1, lanes]
            acc = acc + gap * gap * (prec[i : i + 1, lanes] * ramp)
    parts[sp] = jnp.broadcast_to(jnp.sum(acc, axis=1, keepdims=True), (1, 128))
    for where in mates:
        small(parts.at[sp], parts.at[sp], 1, where).start()

    for j in (1, 2, 3):
        land(moving[j])
        wave(stage, j, True)
    later = ship(a4, 1, (2, 3))
    land(moving[4])
    wave(stage, 4, True)
    later.update(ship(a4, 1, (1, 4)))

    stage2 = (a4, a1, a2, a3, a8)
    inner(stage2, 1, False)

    small(picks.at[pl.ds(0, NPEER - 1)], picks.at[pl.ds(0, NPEER - 1)], 0, after).wait()
    start_second(0)

    for j in (2, 3, 1):
        land(later[j])
    for j in (1, 2, 3):
        wave(stage2, j, False)
    land(later[4])
    wave(stage2, 4, False)
    last = ship(a8, 2, (1,))

    @pl.loop(0, 4)
    def _(i):
        tiles = [a8[i + 4, 8 * k : 8 * k + 8, :] for k in range(4)]
        above = (tiles[1], tiles[2], tiles[3], upper(tiles[0]))
        below = (lower(tiles[3]), tiles[0], tiles[1], tiles[2])
        for k in range(4):
            s = slice(8 * k, 8 * k + 8)
            c = tiles[k]
            put(1, i, k, sv[i, s, :] - 0.5 * (north(c, -1) - north(c, 1)))
            put(2, i, k, sw[i, s, :] - 0.5 * (above[k] - below[k]))

    start_first(1)

    land(last[1])

    @pl.loop(0, 4)
    def _(i):
        for k in range(4):
            s = slice(8 * k, 8 * k + 8)
            put(0, i, k, su[i + 1, s, :] - 0.5 * (a8[i + 5, s, :] - a8[i + 3, s, :]))

    start_first(2)

    small(parts.at[pl.ds(0, 7)], parts.at[pl.ds(0, 7)], 1, after).wait()
    mis = parts[0]
    for k in range(1, 8):
        mis = mis + parts[k]
    totals[me] = -0.5 * mis
    for _, where in peers:
        small(totals.at[me], totals.at[me], 2, where).start()

    start_second(1)

    small(totals.at[pl.ds(0, NPEER - 1)], totals.at[pl.ds(0, NPEER - 1)], 2, after).wait()
    a = totals[0:16]
    b = totals[16:32]
    top = jnp.maximum(a, b)
    isle = top + jnp.log(jnp.exp(a - top) + jnp.exp(b - top))
    peak = jnp.max(isle, axis=0)
    whole = peak + jnp.log(jnp.sum(jnp.exp(isle - peak[None]), axis=0))
    own = totals[isl]
    other = totals[isl + 16]
    top1 = jnp.maximum(own, other)
    mine = top1 + jnp.log(jnp.exp(own - top1) + jnp.exp(other - top1))
    logp[...] = totals[me] - mine
    logi[...] = mine - whole

    start_second(2)

    for f in range(4):
        for edge in edges[f]:
            edge.wait_send()
    for group in (moving, later, last):
        for copies in group.values():
            for copy in copies:
                copy.wait_send()
    for g in range(3):
        all_of(g, s1, r1).wait_send()
        all_of(g, s2, r2).wait()


def step(ensemble, observations, obs_precision, island_ancestor, particle_ancestor):
    field = ensemble[0, 0]
    vmem = pl.BlockSpec(memory_space=pltpu.VMEM)
    smem = pl.BlockSpec(memory_space=pltpu.SMEM)
    far = pl.BlockSpec(memory_space=pl.ANY)
    f32 = jnp.float32
    tall = Z0 + NZ + 8
    dma = pltpu.SemaphoreType.DMA
    out, logp, logi = pl.pallas_call(
        kernel,
        out_shape=(
            pltpu.VMEM(field.shape, f32),
            pltpu.VMEM((1, 128), f32),
            pltpu.VMEM((1, 128), f32),
        ),
        in_specs=[far, smem, far, far, far],
        out_specs=(vmem, vmem, vmem),
        scratch_shapes=[pltpu.VMEM((10, 4, tall, 128), f32) for _ in range(4)]
        + [
            pltpu.VMEM((6, NZ, LANES), f32),
            pltpu.VMEM((4, NZ, LANES), f32),
            pltpu.VMEM((4, NZ, LANES), f32),
        ]
        + [pltpu.VMEM((12, NZ, LANES), f32) for _ in range(6)]
        + [pltpu.VMEM((4, NPEER * 16, 128), f32)]
        + [pltpu.VMEM((NPEER, n, 16, 128), f32) for _, n in GROUPS + GROUPS]
        + [
            pltpu.VMEM((NPEER, 1, 128), f32),
            pltpu.VMEM((8, 1, 128), f32),
            pltpu.VMEM((NPEER, 1, 128), f32),
            pltpu.SMEM((16,), jnp.int32),
            pltpu.VMEM((4, LANES), f32),
            pltpu.VMEM((4, LANES), f32),
            dma((5, 4)),
            dma((4, 2, 4)),
            dma((4, 2, 4)),
            dma((3, 5, 2)),
            dma((3, 5, 2)),
            dma((3,)),
            dma((3,)),
            dma((3,)),
            dma((3,)),
            dma((3,)),
            dma((3,)),
            pltpu.SemaphoreType.REGULAR((3,)),
        ],
        compiler_params=pltpu.CompilerParams(
            collective_id=0, has_side_effects=True, vmem_limit_bytes=56 * 1024 * 1024
        ),
    )(island_ancestor, particle_ancestor, observations, obs_precision, field)
    return out[None, None], logp[:, :1], logi[0, :1]


def solution(mesh):
    return jax.shard_map(
        step,
        mesh=mesh,
        in_specs=(
            P("isl", "par", None, "sp", None, None),
            P("sp", None),
            P("sp", None),
            P(),
            P("isl", "par"),
        ),
        out_specs=(P("isl", "par", None, "sp", None, None), P("isl", "par"), P("isl")),
        check_vma=False,
    )
```

time: 73.3 us -> 71.3 us (0.973)
  Pallas kernels: 68.9 us -> 67.2 us
    pallas_call x1, Pallas kernels: 68.9 us -> 67.2 us  [step(): pl.pallas_call(kernel, out_shape=(pltpu.VMEM(field.shape, f32), pltpu.VME...]
where the time goes in v5:
time: 71.3 us; the launch traced here: 71.2 us
  Pallas kernels  67.2 us (94%)
  between operations  3 us (4%)
  local copies, waits for them, and re-layouts  0.97 us (1%)
    pallas_call x1, Pallas kernels, step(): pl.pallas_call(kernel, out_shape=(pltpu.VMEM(field.shape, f32), pltpu.VME...  67.2 us

profile of v5, /device:TPU:25, one launch (start us, length us, event | category | flops | bytes accessed | tf_op | source)
XLA Modules:
  0.0 71.2 jit_solution(7440949679488958316)
XLA Ops:
  1.3 67.2 %shard_map.76 = (f32[4,4,32,512]{3,2,1,0:T(8,128)S(1)}, f32[1,128]{1,0:T(1,128)S(1)}, f32[1,128]{1,0:T(1,128)S(1)}) custom-call(s32[16]{0:T(128)} %anc_far.1, s32[1,1]{1,0:T(1,128)S(6)} %copy.12.pick, f32[4,512]{1,0:T(4,128)} %obs_far.1, f32[4,512]{1,0:T(4,128)} %prec_far.1, f32[4,4,32,512]{3,2,1,0:T(8,128)} %bitcast.8), custom_call_target="tpu_custom_call" | custom-call | tf_op jit(solution)/shard_map/pallas_call | solution.py:441
  68.5 1.0 %copy.11 = f32[1,1,4,4,32,512]{5,4,3,2,1,0:T(8,128)} copy(f32[1,1,4,4,32,512]{5,4,3,2,1,0:T(8,128)S(1)} %bitcast.5) | data formatting | bytes 2097152

commit v6 on v5

--- a/solution.py
+++ b/solution.py
@@ -7,7 +7,7 @@
 
 MESH = pl.DeviceIdType.MESH
 NPEER = 32
-GROUPS = ((3, 1), (1, 2), (0, 1))
+GROUPS = ((3, 1, 0, 8), (3, 1, 8, 8), (1, 2, 0, 16), (0, 1, 0, 16))
 STEP = 0.2
 VISC = 0.05
 STRAT = 1.0
@@ -49,21 +49,28 @@
     return jnp.where(place == 0, 0.0, pltpu.roll(tile, 1, 0))
 
 
-def chunk_of(ref, first, count, flat):
+def chunk_of(ref, group, flat):
+    field, count, first, levels = group
     row = flat // 8
     lane = pl.multiple_of((flat // 2) % 4 * 128, 128)
-    start = pl.multiple_of(flat % 2 * 16, 16)
-    return ref.at[pl.ds(first, count), row, pl.ds(start, 16), pl.ds(lane, 128)]
+    start = pl.multiple_of(flat % 2 * 16 + first, 8)
+    return ref.at[pl.ds(field, count), row, pl.ds(start, levels), pl.ds(lane, 128)]
+
+
+def piece_of(ref, group, flat):
+    field, count, first, levels = group
+    start = pl.multiple_of(flat * 16 + first, 8)
+    return ref.at[pl.ds(field, count), pl.ds(start, levels), :]
 
 
 def kernel(
     anc_far, pick, obs_far, prec_far, ens, out, logp, logi,
     xu, xv, xw, xb, su, sv, sw, dv, a1, a2, a3, a4, a8, fore,
-    h0, h1, h2, g0, g1, g2, picks, parts, totals,
+    h0, h1, h2, h3, g0, g1, g2, g3, picks, parts, totals,
     anc, obs, prec, lsem, hs, hr, ws, wr, s1, r1, s2, r2, ssem, rsem, met,
 ):
-    held = (h0, h1, h2)
-    sent = (g0, g1, g2)
+    held = (h0, h1, h2, h3)
+    sent = (g0, g1, g2, g3)
     isl = lax.axis_index("isl")
     par = lax.axis_index("par")
     sp = lax.axis_index("sp")
@@ -123,19 +130,24 @@
     pl.semaphore_wait(barrier, len(close))
 
     edges = {}
-    for f in (3, 1, 2, 0):
-        w = 3 if f == 0 else 2
-        edges[f] = []
+    for e, f, near, far_ in ((3, 3, 0, 2), (1, 1, 0, 2), (2, 2, 0, 2), (0, 0, 0, 2), (4, 0, 2, 3)):
+        edges[e] = []
         for lane in range(4):
             cut = pl.ds(lane * 128, 128)
             into = fields[f].at[:, lane, Z0 : Z0 + NZ, :]
-            edges[f] += [
+            edges[e] += [
                 remote(
-                    ens.at[f, 4 - w : 4, :, cut], into.at[3 - w : 3], hs.at[f, 0, lane], hr.at[f, 0, lane], after
+                    ens.at[f, 4 - far_ : 4 - near, :, cut],
+                    into.at[3 - far_ : 3 - near],
+                    hs.at[e, 0, lane],
+                    hr.at[e, 0, lane],
+                    after,
                 ),
-                remote(ens.at[f, 0:w, :, cut], into.at[7 : 7 + w], hs.at[f, 1, lane], hr.at[f, 1, lane], before),
+                remote(
+                    ens.at[f, near:far_, :, cut], into.at[7 + near : 7 + far_], hs.at[e, 1, lane], hr.at[e, 1, lane], before
+                ),
             ]
-        for edge in edges[f]:
+        for edge in edges[e]:
             edge.start()
 
     rounds = (
@@ -196,12 +208,10 @@
         return tuple(level(q, r, k, 0) * (STEP / 12.0) for q in (xu, xv, xw))
 
     def first_copy(g, flat, where):
-        f, n = GROUPS[g]
-        return remote(fore.at[pl.ds(f, n), pl.ds(pl.multiple_of(flat * 16, 16), 16), :], held[g].at[me], s1.at[g], r1.at[g], where)
+        return remote(piece_of(fore, GROUPS[g], flat), held[g].at[me], s1.at[g], r1.at[g], where)
 
     def second_copy(g, flat, where):
-        f, n = GROUPS[g]
-        return remote(sent[g].at[flat], chunk_of(out, f, n, me), s2.at[g], r2.at[g], where)
+        return remote(sent[g].at[flat], chunk_of(out, GROUPS[g], me), s2.at[g], r2.at[g], where)
 
     def all_of(g, s, r):
         return remote(
@@ -209,24 +219,22 @@
         )
 
     def start_first(g):
-        f, n = GROUPS[g]
         for flat, where in peers:
             first_copy(g, flat, where).start()
-        held[g][me] = fore[pl.ds(f, n), pl.ds(pl.multiple_of(me * 16, 16), 16), :]
+        held[g][me] = piece_of(fore, GROUPS[g], me)[...]
 
     def start_second(g):
-        f, n = GROUPS[g]
         all_of(g, s1, r1).wait_recv()
 
         @pl.loop(0, NPEER)
         def _(d):
             src = anc[lax.rem(d, 16)]
-            choose = jnp.broadcast_to(picks[d][None], (n, 16, 128)) < 0.5
+            choose = jnp.broadcast_to(picks[d][None], held[g].shape[1:]) < 0.5
             sent[g][d] = jnp.where(choose, held[g][src], held[g][src + 16])
 
         for flat, where in peers:
             second_copy(g, flat, where).start()
-        chunk_of(out, f, n, me)[...] = sent[g][me]
+        chunk_of(out, GROUPS[g], me)[...] = sent[g][me]
 
     for load in loads:
         load.wait()
@@ -241,9 +249,10 @@
             put(3, i, k, c + g - (STEP * STRAT) * level(xw, r, k, 0))
 
     hear(2)
-    start_first(0)
     for _, where in peers:
         small(picks.at[me], picks.at[me], 0, where).start()
+    start_first(0)
+    start_first(1)
 
     land(edges[1])
 
@@ -274,20 +283,6 @@
             dv[i + 4, 8 * k : 8 * k + 8, :] = dv[i + 4, 8 * k : 8 * k + 8, :] + 0.5 * (above[k] - below[k])
 
     land(edges[0])
-
-    @pl.loop(0, 6)
-    def _(i):
-        r = i + 2
-        for k in range(4):
-            u, v, w = winds(r, k)
-            c, g = tendency(xu, r, k, u, v, w)
-            su[i, 8 * k : 8 * k + 8, :] = c + g
-
-    @pl.loop(0, 4)
-    def _(i):
-        for k in range(4):
-            s = slice(8 * k, 8 * k + 8)
-            dv[i + 4, s, :] = dv[i + 4, s, :] + 0.5 * (su[i + 2, s, :] - su[i, s, :])
 
     def ship(buf, e, away_rows):
         copies = {}
@@ -304,6 +299,34 @@
                 copy.start()
         return copies
 
+    def star_u(i):
+        r = i + 2
+        for k in range(4):
+            u, v, w = winds(r, k)
+            c, g = tendency(xu, r, k, u, v, w)
+            su[i, 8 * k : 8 * k + 8, :] = c + g
+
+    def add_x(i):
+        for k in range(4):
+            s = slice(8 * k, 8 * k + 8)
+            dv[i + 4, s, :] = dv[i + 4, s, :] + 0.5 * (su[i + 2, s, :] - su[i, s, :])
+
+    @pl.loop(1, 5)
+    def _(i):
+        star_u(i)
+
+    add_x(1)
+    add_x(2)
+    moving = ship(dv, 0, (2,))
+    land(edges[4])
+
+    @pl.loop(0, 2)
+    def _(side):
+        star_u(side * 5)
+
+    add_x(0)
+    add_x(3)
+
     def sweep_row(src, dst, row, first):
         tiles = [src[row, 8 * k : 8 * k + 8, :] for k in range(4)]
         above = (tiles[1], tiles[2], tiles[3], upper(tiles[0]))
@@ -332,7 +355,7 @@
             inner(levels, j + 1, first)
 
     stage = (dv, a1, a2, a3, a4)
-    moving = ship(dv, 0, (1, 2, 3, 4))
+    moving.update(ship(dv, 0, (1, 3, 4)))
     inner(stage, 1, True)
 
     acc = jnp.zeros((1, 128), jnp.float32)
@@ -351,6 +374,8 @@
         land(moving[j])
         wave(stage, j, True)
     later = ship(a4, 1, (2, 3))
+    small(picks.at[pl.ds(0, NPEER - 1)], picks.at[pl.ds(0, NPEER - 1)], 0, after).wait()
+    start_second(0)
     land(moving[4])
     wave(stage, 4, True)
     later.update(ship(a4, 1, (1, 4)))
@@ -358,8 +383,7 @@
     stage2 = (a4, a1, a2, a3, a8)
     inner(stage2, 1, False)
 
-    small(picks.at[pl.ds(0, NPEER - 1)], picks.at[pl.ds(0, NPEER - 1)], 0, after).wait()
-    start_second(0)
+    start_second(1)
 
     for j in (2, 3, 1):
         land(later[j])
@@ -380,7 +404,7 @@
             put(1, i, k, sv[i, s, :] - 0.5 * (north(c, -1) - north(c, 1)))
             put(2, i, k, sw[i, s, :] - 0.5 * (above[k] - below[k]))
 
-    start_first(1)
+    start_first(2)
 
     land(last[1])
 
@@ -390,7 +414,7 @@
             s = slice(8 * k, 8 * k + 8)
             put(0, i, k, su[i + 1, s, :] - 0.5 * (a8[i + 5, s, :] - a8[i + 3, s, :]))
 
-    start_first(2)
+    start_first(3)
 
     small(parts.at[pl.ds(0, 7)], parts.at[pl.ds(0, 7)], 1, after).wait()
     mis = parts[0]
@@ -400,7 +424,7 @@
     for _, where in peers:
         small(totals.at[me], totals.at[me], 2, where).start()
 
-    start_second(1)
+    start_second(2)
 
     small(totals.at[pl.ds(0, NPEER - 1)], totals.at[pl.ds(0, NPEER - 1)], 2, after).wait()
     a = totals[0:16]
@@ -416,16 +440,16 @@
     logp[...] = totals[me] - mine
     logi[...] = mine - whole
 
-    start_second(2)
-
-    for f in range(4):
+    start_second(3)
+
+    for f in range(5):
         for edge in edges[f]:
             edge.wait_send()
     for group in (moving, later, last):
         for copies in group.values():
             for copy in copies:
                 copy.wait_send()
-    for g in range(3):
+    for g in range(len(GROUPS)):
         all_of(g, s1, r1).wait_send()
         all_of(g, s2, r2).wait()
 
@@ -455,7 +479,7 @@
         ]
         + [pltpu.VMEM((12, NZ, LANES), f32) for _ in range(6)]
         + [pltpu.VMEM((4, NPEER * 16, 128), f32)]
-        + [pltpu.VMEM((NPEER, n, 16, 128), f32) for _, n in GROUPS + GROUPS]
+        + [pltpu.VMEM((NPEER, n, levels, 128), f32) for _, n, _, levels in GROUPS + GROUPS]
         + [
             pltpu.VMEM((NPEER, 1, 128), f32),
             pltpu.VMEM((8, 1, 128), f32),
@@ -464,14 +488,14 @@
             pltpu.VMEM((4, LANES), f32),
             pltpu.VMEM((4, LANES), f32),
             dma((5, 4)),
-            dma((4, 2, 4)),
-            dma((4, 2, 4)),
+            dma((5, 2, 4)),
+            dma((5, 2, 4)),
             dma((3, 5, 2)),
             dma((3, 5, 2)),
-            dma((3,)),
-            dma((3,)),
-            dma((3,)),
-            dma((3,)),
+            dma((4,)),
+            dma((4,)),
+            dma((4,)),
+            dma((4,)),
             dma((3,)),
             dma((3,)),
             pltpu.SemaphoreType.REGULAR((3,)),

time: 71.3 us -> 69.8 us (0.979)
  Pallas kernels: 67.2 us -> 65.7 us
    pallas_call x1, Pallas kernels: 67.2 us -> 65.7 us  [step(): pl.pallas_call(kernel, out_shape=(pltpu.VMEM(field.shape, f32), pltpu.VME...]
where the time goes in v6:
time: 69.8 us; the launch traced here: 69.7 us
  Pallas kernels  65.7 us (94%)
  between operations  3 us (4%)
  local copies, waits for them, and re-layouts  0.97 us (1%)
    pallas_call x1, Pallas kernels, step(): pl.pallas_call(kernel, out_shape=(pltpu.VMEM(field.shape, f32), pltpu.VME...  65.7 us

profile of v6, /device:TPU:25, one launch (start us, length us, event | category | flops | bytes accessed | tf_op | source)
XLA Modules:
  0.0 69.7 jit_solution(8633956245752207012)
XLA Ops:
  1.3 65.7 %shard_map.76 = (f32[4,4,32,512]{3,2,1,0:T(8,128)S(1)}, f32[1,128]{1,0:T(1,128)S(1)}, f32[1,128]{1,0:T(1,128)S(1)}) custom-call(s32[16]{0:T(128)} %anc_far.1, s32[1,1]{1,0:T(1,128)S(6)} %copy.12.pick, f32[4,512]{1,0:T(4,128)} %obs_far.1, f32[4,512]{1,0:T(4,128)} %prec_far.1, f32[4,4,32,512]{3,2,1,0:T(8,128)} %bitcast.8), custom_call_target="tpu_custom_call" | custom-call | tf_op jit(solution)/shard_map/pallas_call | solution.py:465
  67.0 1.0 %copy.11 = f32[1,1,4,4,32,512]{5,4,3,2,1,0:T(8,128)} copy(f32[1,1,4,4,32,512]{5,4,3,2,1,0:T(8,128)S(1)} %bitcast.5) | data formatting | bytes 2097152

commit v7 on v6

--- a/solution.py
+++ b/solution.py
@@ -240,13 +240,17 @@
         load.wait()
     land(edges[3])
 
-    @pl.loop(0, 4)
-    def _(i):
+    def star_b(i):
         r = i + 3
         for k in range(4):
             u, v, w = winds(r, k)
             c, g = tendency(xb, r, k, u, v, w)
             put(3, i, k, c + g - (STEP * STRAT) * level(xw, r, k, 0))
+
+    @pl.loop(0, 2)
+    def _(i):
+        star_b(2 * i)
+        star_b(2 * i + 1)
 
     hear(2)
     for _, where in peers:
@@ -311,18 +315,18 @@
             s = slice(8 * k, 8 * k + 8)
             dv[i + 4, s, :] = dv[i + 4, s, :] + 0.5 * (su[i + 2, s, :] - su[i, s, :])
 
-    @pl.loop(1, 5)
+    @pl.loop(0, 2)
     def _(i):
-        star_u(i)
+        star_u(2 * i + 1)
+        star_u(2 * i + 2)
 
     add_x(1)
     add_x(2)
     moving = ship(dv, 0, (2,))
     land(edges[4])
 
-    @pl.loop(0, 2)
-    def _(side):
-        star_u(side * 5)
+    star_u(0)
+    star_u(5)
 
     add_x(0)
     add_x(3)

time: 69.8 us -> 69.6 us (level)
  no operation moved by 1% of the time
where the time goes in v7:
time: 69.6 us; the launch traced here: 69.5 us
  Pallas kernels  65.5 us (94%)
  between operations  3 us (4%)
  local copies, waits for them, and re-layouts  0.97 us (1%)
    pallas_call x1, Pallas kernels, step(): pl.pallas_call(kernel, out_shape=(pltpu.VMEM(field.shape, f32), pltpu.VME...  65.5 us

profile of v7, /device:TPU:25, one launch (start us, length us, event | category | flops | bytes accessed | tf_op | source)
XLA Modules:
  0.0 69.5 jit_solution(5490367008974332235)
XLA Ops:
  1.3 65.5 %shard_map.76 = (f32[4,4,32,512]{3,2,1,0:T(8,128)S(1)}, f32[1,128]{1,0:T(1,128)S(1)}, f32[1,128]{1,0:T(1,128)S(1)}) custom-call(s32[16]{0:T(128)} %anc_far.1, s32[1,1]{1,0:T(1,128)S(6)} %copy.12.pick, f32[4,512]{1,0:T(4,128)} %obs_far.1, f32[4,512]{1,0:T(4,128)} %prec_far.1, f32[4,4,32,512]{3,2,1,0:T(8,128)} %bitcast.8), custom_call_target="tpu_custom_call" | custom-call | tf_op jit(solution)/shard_map/pallas_call | solution.py:469
  66.8 1.0 %copy.11 = f32[1,1,4,4,32,512]{5,4,3,2,1,0:T(8,128)} copy(f32[1,1,4,4,32,512]{5,4,3,2,1,0:T(8,128)S(1)} %bitcast.5) | data formatting | bytes 2097152
